TPU v7x, 32 devices: a whole 2x2x4 slice. The times are simulated.
32 devices in a mesh: groups: 2 (over y), row: 4 (over z), col: 4 (over x, core).
Axes of the slice: x: 2, y: 2, z: 4, core: 2. Of those that a mesh axis runs over, the one named last changes fastest.
Arguments:
- seq_feat: bfloat16 [64, 256], P(('groups', 'row', 'col')), parts along dimension 0, may hold values from -6 to 6
- lengths: int32 [4], P('groups'), parts along dimension 0, may hold values from 1 to 24, 32 in all
- embed_weight: bfloat16 [2, 256, 128], replicated, may hold values from -0.375 to 0.375
- norm_gain: float32 [4, 128], replicated, may hold values from 0.1 to 1.9
- conv_weight: bfloat16 [4, 3, 3, 128, 128], replicated, may hold values from -0.1875 to 0.1875
- proj_weight: bfloat16 [4, 128, 128], replicated, may hold values from -0.5 to 0.5
- pair_cotangent: bfloat16 [64, 32, 128], P(('groups', 'row'), 'col'), parts along dimension 0, may hold values from -13 to 13
Outputs:
- pair_output: bfloat16 [64, 32, 128], P(('groups', 'row'), 'col'), parts along dimension 0
- seq_grad: float32 [64, 256], P(('groups', 'row', 'col')), parts along dimension 0
- embed_grad: float32 [4, 256, 128], P('groups'), parts along dimension 0
- gain_grad: float32 [8, 128], P('groups'), parts along dimension 0
- conv_grad: float32 [8, 3, 3, 128, 128], P('groups'), parts along dimension 0
- proj_grad: float32 [8, 128, 128], P('groups'), parts along dimension 0
There are 2 independent parts, one for each index of `groups`. A program takes and returns all parts, laid end to end along the dimension named above; an argument that names none is the same for every part. Nothing has to cross between parts.
Inputs may be any that keep to these rules, and one draw needn't show every extreme that they name: lengths[0] residues are real; those at and after index lengths[0] are padding; the two entries sum to 32.
All inputs are finite; a program needn't handle non-finite values.
Results may differ from a plain program's by a relative error of at most 0.014.
Values may be sent and summed in bfloat16 or wider, within the bound.
No kernel may reach another device: no remote copies, remote signals or barrier semaphores. Data moves between devices by JAX's collectives and lax.ppermute only.
A program may use at most 64 MiB of HBM per device.

v0:
```python
import math

import jax
import jax.numpy as jnp
from jax import lax
from jax.sharding import PartitionSpec as P

LAYERS = 4


eps = 1e-05


def with_halo(x, sides, width):
    for axis, dim in sides:
        count, length = (lax.axis_size(axis), x.shape[dim])
        up = [(i, (i + 1) % count) for i in range(count - 1)]
        down = [(j, i) for i, j in up]
        last = lax.slice_in_dim(x, length - width, length, axis=dim)
        first = lax.slice_in_dim(x, 0, width, axis=dim)
        before = lax.ppermute(last, axis, up)
        after = lax.ppermute(first, axis, down)
        x = jnp.concatenate([before, x, after], axis=dim)
    return x


def elu_slope(values):
    return jnp.where(values > 0, 1.0, jnp.exp(jnp.minimum(values, 0.0)))


def normalize(stream, gain_row):
    average = jnp.mean(stream, axis=-1, keepdims=True)
    centred = stream - average
    variance = jnp.mean(centred * centred, axis=-1, keepdims=True)
    inv_std = lax.rsqrt(variance + eps)
    normalized = centred * inv_std
    return (normalized, inv_std, normalized * gain_row)


def conv_forward(padded, weight, spacing, height, width):
    channels = padded.shape[-1]
    summed = jnp.zeros((height * width, weight.shape[-1]), jnp.float32)
    for tap_row in range(3):
        for tap_col in range(3):
            window = padded[
                tap_row * spacing : tap_row * spacing + height,
                tap_col * spacing : tap_col * spacing + width,
                :,
            ]
            summed = summed + jnp.dot(
                window.reshape(height * width, channels),
                weight[tap_row, tap_col],
                preferred_element_type=jnp.float32,
            )
    return summed.reshape(height, width, -1)


def conv_backward(padded, weight, spacing, height, width):
    channels = padded.shape[-1]
    summed = jnp.zeros((height * width, weight.shape[-2]), jnp.float32)
    for tap_row in range(3):
        for tap_col in range(3):
            start_row = (2 - tap_row) * spacing
            start_col = (2 - tap_col) * spacing
            window = padded[start_row : start_row + height, start_col : start_col + width, :]
            summed = summed + jnp.dot(
                window.reshape(height * width, channels),
                weight[tap_row, tap_col].T,
                preferred_element_type=jnp.float32,
            )
    return summed.reshape(height, width, -1)


def conv_weight_grad(padded, grad_tile, spacing, height, width):
    channels = padded.shape[-1]
    flat_grad = grad_tile.reshape(height * width, -1)
    terms = []
    for tap_row in range(3):
        row_terms = []
        for tap_col in range(3):
            window = padded[
                tap_row * spacing : tap_row * spacing + height,
                tap_col * spacing : tap_col * spacing + width,
                :,
            ]
            row_terms.append(
                lax.dot_general(
                    window.reshape(height * width, channels),
                    flat_grad,
                    (((0,), (0,)), ((), ())),
                    preferred_element_type=jnp.float32,
                )
            )
        terms.append(jnp.stack(row_terms))
    return jnp.stack(terms)


def body(seq_feat, lengths, embed_weight, norm_gain, conv_weight, proj_weight, pair_cotangent):
    tile_rows = pair_cotangent.shape[0]
    tile_cols = pair_cotangent.shape[1]
    channels = pair_cotangent.shape[2]
    residues = tile_rows * lax.axis_size("row")
    row_start = lax.axis_index("row") * tile_rows
    col_start = lax.axis_index("col") * tile_cols
    row_live = (row_start + jnp.arange(tile_rows, dtype=jnp.int32) < lengths[0]).astype(jnp.float32)
    col_live = (col_start + jnp.arange(tile_cols, dtype=jnp.int32) < lengths[0]).astype(jnp.float32)
    live_mask = row_live[:, None, None] * col_live[None, :, None]
    gathered = lax.all_gather(seq_feat, ("row", "col"), axis=0, tiled=True)
    row_part = lax.dynamic_slice_in_dim(gathered, row_start, tile_rows, 0)
    col_part = lax.dynamic_slice_in_dim(gathered, col_start, tile_cols, 0)
    row_emb = jnp.dot(row_part, embed_weight[0], preferred_element_type=jnp.float32).astype(
        jnp.bfloat16
    )
    col_emb = jnp.dot(col_part, embed_weight[1], preferred_element_type=jnp.float32).astype(
        jnp.bfloat16
    )
    stream = live_mask * (
        row_emb.astype(jnp.float32)[:, None, :] + col_emb.astype(jnp.float32)[None, :, :]
    )
    stored = []
    for layer_number in range(LAYERS):
        spacing = 2**layer_number
        normalized, inv_std, scaled = normalize(stream, norm_gain[layer_number])
        squashed = (live_mask * jax.nn.elu(scaled)).astype(jnp.bfloat16)
        padded = with_halo(squashed, (("row", 0), ("col", 1)), spacing)
        convolved = conv_forward(padded, conv_weight[layer_number], spacing, tile_rows, tile_cols)
        excited = jax.nn.elu(convolved).astype(jnp.bfloat16)
        update = jnp.dot(
            excited.reshape(-1, channels),
            proj_weight[layer_number],
            preferred_element_type=jnp.float32,
        ).reshape(tile_rows, tile_cols, channels)
        stored.append((stream, padded, convolved, excited))
        stream = stream + live_mask * update
    pair_output = stream.astype(jnp.bfloat16)
    grad_scale = 1.0 / residues
    back_grad = pair_cotangent.astype(jnp.float32)
    gain_terms = [None] * LAYERS
    conv_terms = [None] * LAYERS
    proj_terms = [None] * LAYERS
    for layer_number in reversed(range(LAYERS)):
        spacing = 2**layer_number
        old_stream, padded, convolved, excited = stored[layer_number]
        masked = (live_mask * back_grad).astype(jnp.bfloat16)
        flat_masked = masked.reshape(-1, channels)
        proj_term = (
            lax.dot_general(
                excited.reshape(-1, channels),
                flat_masked,
                (((0,), (0,)), ((), ())),
                preferred_element_type=jnp.float32,
            )
            * grad_scale
        )
        d_excited = jnp.dot(
            flat_masked, proj_weight[layer_number].T, preferred_element_type=jnp.float32
        ).reshape(tile_rows, tile_cols, channels)
        d_pre = (d_excited * elu_slope(convolved)).astype(jnp.bfloat16)
        conv_term = conv_weight_grad(padded, d_pre, spacing, tile_rows, tile_cols) * grad_scale
        d_padded = with_halo(d_pre, (("row", 0), ("col", 1)), spacing)
        d_squashed = conv_backward(
            d_padded, conv_weight[layer_number], spacing, tile_rows, tile_cols
        )
        normalized, inv_std, scaled = normalize(old_stream, norm_gain[layer_number])
        d_scaled = live_mask * d_squashed * elu_slope(scaled)
        gain_term = jnp.sum(d_scaled * normalized, axis=(0, 1)) * grad_scale
        d_norm = d_scaled * norm_gain[layer_number]
        back_grad = back_grad + inv_std * (
            d_norm
            - jnp.mean(d_norm, axis=-1, keepdims=True)
            - normalized * jnp.mean(d_norm * normalized, axis=-1, keepdims=True)
        )
        gain_terms[layer_number] = gain_term
        conv_terms[layer_number] = conv_term
        proj_terms[layer_number] = proj_term
    final_masked = live_mask * back_grad
    row_totals = jnp.sum(final_masked, axis=1)
    col_totals = jnp.sum(final_masked, axis=0)
    d_row = lax.psum_scatter(row_totals, "col", scatter_dimension=0, tiled=True).astype(
        jnp.bfloat16
    )
    spread_cols = lax.dynamic_update_slice_in_dim(
        jnp.zeros((residues, channels), jnp.float32), col_totals, col_start, 0
    )
    d_col = lax.psum_scatter(spread_cols, ("row", "col"), scatter_dimension=0, tiled=True).astype(
        jnp.bfloat16
    )
    seq_grad = (
        jnp.dot(d_row, embed_weight[0].T, preferred_element_type=jnp.float32)
        + jnp.dot(d_col, embed_weight[1].T, preferred_element_type=jnp.float32)
    ) / math.sqrt(residues)
    embed_term = (
        jnp.stack(
            [
                lax.dot_general(
                    seq_feat, d_row, (((0,), (0,)), ((), ())), preferred_element_type=jnp.float32
                ),
                lax.dot_general(
                    seq_feat, d_col, (((0,), (0,)), ((), ())), preferred_element_type=jnp.float32
                ),
            ]
        )
        * grad_scale
    )
    gain_grad = jnp.stack(gain_terms)
    conv_grad = jnp.stack(conv_terms)
    proj_grad = jnp.stack(proj_terms)
    gain_grad, conv_grad, proj_grad, embed_grad = lax.psum(
        (gain_grad, conv_grad, proj_grad, embed_term), ("row", "col")
    )
    return (pair_output, seq_grad, embed_grad, gain_grad, conv_grad, proj_grad)


def solution(mesh):
    placed = (
        P(("groups", "row", "col"), None),
        P("groups"),
        P(),
        P(),
        P(),
        P(),
        P(("groups", "row"), "col", None),
    )
    return jax.shard_map(
        body,
        mesh=mesh,
        in_specs=placed,
        out_specs=(
            P(("groups", "row"), "col", None),
            P(("groups", "row", "col"), None),
            P("groups", None, None),
            P("groups", None),
            P("groups", None, None, None, None),
            P("groups", None, None),
        ),
        check_vma=False,
    )
```

profile of v0, /device:TPU:0, one launch (start us, length us, event | category | flops | bytes accessed | tf_op | source)
XLA Modules:
  0.0 350.0 jit_solution(10148906690786767600)
XLA Ops:
  8.8 23.3 %all-gather = bf16[16,2,256]{2,1,0:T(2,128)(2,1)S(1)} all-gather(bf16[1,2,256]{2,1,0:T(2,128)(2,1)} %bitcast.781), channel_id=1, replica_groups=mesh['groups'=2,'row'=4,'col'=4] {'row','col'}, dimensions={0}, use_global_device_ids=true | all-gather | bytes 17408 | tf_op jit(solution)/shard_map/all_gather | solution.py:108
  35.9 1.3 collective-permute-start.1
  37.2 1.3 slice_bitcast_fusion
  38.5 2.9 collective-permute-done.1
  42.7 1.3 collective-permute-start.3
  44.1 1.6 collective-permute-done.3
  47.4 2.4 collective-permute-start.4
  49.7 1.3 collective-permute-start.5
  53.9 1.3 collective-permute-done.5
  55.3 2.6 collective-permute-start.6
  57.9 1.3 collective-permute-start.7
  59.3 2.4 collective-permute-done.7
  63.3 3.9 %collective-permute-start.8 = (bf16[4,8,128]{2,1,0:T(8,128)(2,1)S(1)}, bf16[4,8,128]{2,1,0:T(8,128)(2,1)S(1)}, u32[]{:S(2)}, u32[]{:S(2)}) collective-permute-start(bf16[4,8,128]{2,1,0:T(8,128)(2,1)S(1)} %get-tuple-element.67), channel_id=1, source_target_pairs={{0,4},{4,8},{8,12},{1,5},{5,9},{9,13},{2,6},{6,10},{10,14},{3,7},{... | collective-permute-start | bytes 24584 | tf_op jit(solution)/shard_map/ppermute | solution.py:21
  67.2 1.3 collective-permute-start.9
  68.6 4.1 %collective-permute-done.9 = bf16[4,8,128]{2,1,0:T(8,128)(2,1)S(1)} collective-permute-done((bf16[4,8,128]{2,1,0:T(8,128)(2,1)S(1)}, bf16[4,8,128]{2,1,0:T(8,128)(2,1)S(1)}, u32[]{:S(2)}, u32[]{:S(2)}) %collective-permute-start.9) | collective-permute-done | bytes 8224 | tf_op jit(solution)/shard_map/ppermute | solution.py:22
  72.8 2.9 collective-permute-start.10
  75.6 1.3 collective-permute-start.11
  77.2 2.5 collective-permute-done.11
  81.0 1.3 collective-permute-start.13
  82.3 4.5 %collective-permute-start.12 = (bf16[8,8,128]{2,1,0:T(8,128)(2,1)S(1)}, bf16[8,8,128]{2,1,0:T(8,128)(2,1)S(1)}, u32[]{:S(2)}, u32[]{:S(2)}) collective-permute-start(bf16[8,8,128]{2,1,0:T(8,128)(2,1)S(1)} %fusion.106), channel_id=1, source_target_pairs={{0,4},{4,8},{8,12},{1,5},{5,9},{9,13},{2,6},{6,10},{10,14},{3,7},{... | collective-permute-start | bytes 49160 | tf_op jit(solution)/shard_map/ppermute | solution.py:21
  87.0 1.3 collective-permute-done.12
  89.6 3.9 %collective-permute-start.14 = (bf16[24,8,128]{2,1,0:T(8,128)(2,1)S(1)}, bf16[24,8,128]{2,1,0:T(8,128)(2,1)S(1)}, u32[]{:S(2)}, u32[]{:S(2)}) collective-permute-start(bf16[24,8,128]{2,1,0:T(8,128)(2,1)S(1)} %pad_maximum_fusion.3), channel_id=1, source_target_pairs={{0,1},{1,2},{2,3},{4,5},{5,6},{6,7},{8,9},{9,10},{10,11},{12,13},{... | collective-permute-start | bytes 147464 | tf_op jit(solution)/shard_map/ppermute | solution.py:21
  95.1 1.3 collective-permute-start.17
  96.4 4.5 %collective-permute-start.16 = (bf16[8,8,128]{2,1,0:T(8,128)(2,1)S(1)}, bf16[8,8,128]{2,1,0:T(8,128)(2,1)S(1)}, u32[]{:S(2)}, u32[]{:S(2)}) collective-permute-start(bf16[8,8,128]{2,1,0:T(8,128)(2,1)S(1)} %fusion.50), channel_id=1, source_target_pairs={{0,4},{4,8},{8,12},{1,5},{5,9},{9,13},{2,6},{6,10},{10,14},{3,7},{... | collective-permute-start | bytes 49160 | tf_op jit(solution)/shard_map/ppermute | solution.py:21
  103.4 3.6 %collective-permute-start.19 = (bf16[24,8,128]{2,1,0:T(8,128)(2,1)S(1)}, bf16[24,8,128]{2,1,0:T(8,128)(2,1)S(1)}, u32[]{:S(2)}, u32[]{:S(2)}) collective-permute-start(bf16[24,8,128]{2,1,0:T(8,128)(2,1)S(1)} %pad_maximum_fusion.4), channel_id=1, source_target_pairs={{0,1},{1,2},{2,3},{4,5},{5,6},{6,7},{8,9},{9,10},{10,11},{12,13},{... | collective-permute-start | bytes 147464 | tf_op jit(solution)/shard_map/ppermute | solution.py:21
  107.1 1.3 collective-permute-start.18
  109.0 3.4 collective-permute-done.18
  113.7 3.9 %collective-permute-start.20 = (bf16[4,8,128]{2,1,0:T(8,128)(2,1)S(1)}, bf16[4,8,128]{2,1,0:T(8,128)(2,1)S(1)}, u32[]{:S(2)}, u32[]{:S(2)}) collective-permute-start(bf16[4,8,128]{2,1,0:T(8,128)(2,1)S(1)} %get-tuple-element.65), channel_id=1, source_target_pairs={{0,4},{4,8},{8,12},{1,5},{5,9},{9,13},{2,6},{6,10},{10,14},{3,7},{... | collective-permute-start | bytes 24584 | tf_op jit(solution)/shard_map/ppermute | solution.py:21
  117.7 1.3 collective-permute-start.21
  121.1 2.1 collective-permute-done.21
  123.2 1.3 collective-permute-start.22
  124.5 3.9 %collective-permute-start.23 = (bf16[16,4,128]{2,1,0:T(4,128)(2,1)S(1)}, bf16[16,4,128]{2,1,0:T(4,128)(2,1)S(1)}, u32[]{:S(2)}, u32[]{:S(2)}) collective-permute-start(bf16[16,4,128]{2,1,0:T(4,128)(2,1)S(1)} %get-tuple-element.42), channel_id=1, source_target_pairs={{0,1},{1,2},{2,3},{4,5},{5,6},{6,7},{8,9},{9,10},{10,11},{12,13},{... | collective-permute-start | bytes 49160 | tf_op jit(solution)/shard_map/ppermute | solution.py:21
  132.1 3.3 collective-permute-start.24
  135.4 1.3 collective-permute-start.25
  137.5 3.4 collective-permute-done.25
  140.9 1.3 collective-permute-start.26
  142.2 3.0 collective-permute-start.27
  149.5 3.3 collective-permute-start.28
  152.8 1.3 collective-permute-start.29
  154.6 1.6 pad_maximum_fusion
  156.9 1.3 collective-permute-done.29
  158.3 1.3 collective-permute-start.30
  159.6 4.6 %collective-permute-start.31 = (bf16[10,1,128]{2,1,0:T(2,128)(2,1)S(1)}, bf16[10,1,128]{2,1,0:T(2,128)(2,1)S(1)}, u32[]{:S(2)}, u32[]{:S(2)}) collective-permute-start(bf16[10,1,128]{2,1,0:T(2,128)(2,1)S(1)} %get-tuple-element.56), channel_id=1, source_target_pairs={{0,1},{1,2},{2,3},{4,5},{5,6},{6,7},{8,9},{9,10},{10,11},{12,13},{... | collective-permute-start | bytes 7688 | tf_op jit(solution)/shard_map/ppermute | solution.py:21
  166.7 9.7 %all-reduce = bf16[8,128]{1,0:T(8,128)(2,1)S(1)} all-reduce(f32[8,128]{1,0:T(8,128)S(1)} %get-tuple-element.31), channel_id=2, replica_groups=mesh['groups'=2,'row'=4,'col'=4] {'col'}, use_global_device_ids=true, to_apply=%region_17.18.clone | all-reduce | flops 1024 | bytes 6144
  176.4 59.6 %all-reduce.2 = (bf16[32,128]{1,0:T(8,128)(2,1)S(1)}, f32[4,128]{1,0:T(4,128)}) all-reduce(f32[32,128]{1,0:T(8,128)S(1)} %constant_dynamic-update-slice_fusion, f32[4,128]{1,0:T(4,128)S(1)} %pad_maximum_fusion.48), channel_id=3, replica_groups=mesh['groups'=2,'row'=4,'col'=4] {'row','col'}, use_global_device_ids=true, to_apply=%region_19.20.clone | all-reduce | flops 4608 | bytes 28672
  238.9 98.4 %all-reduce.6.cloned.1.call-done = (f32[2,256,128]{1,2,0:T(8,128)}, f32[4,3,3,128,128]{4,3,2,1,0:T(8,128)}, f32[4,128,128]{2,1,0:T(8,128)}) async-done(((f32[2,256,128]{1,2,0:T(8,128)}, f32[4,3,3,128,128]{4,3,2,1,0:T(8,128)}, f32[4,128,128]{2,1,0:T(8,128)}), (f32[2,256,128]{1,2,0:T(8,128)}, f32[4,3,3,128,128]{4,3,2,1,0:T(8,128)}, f32[4,128,128]{2,1,0:T(8,128)})) %all-reduce.6.cloned.1.call-update) | async-done | bytes 2883600 | tf_op jit(solution)/shard_map/psum | solution.py:208
  337.3 1.8 copy.14
  339.1 3.4 copy.19
  (256 shorter events, 38.6 us)
Async XLA Ops:
  7.2 44.0 %copy-start.6 = (u32[32]{0:T(128)S(1)}, u32[32]{0:T(128)}, u32[]{:S(2)}) copy-start(u32[32]{0:T(128)} %constant.72) | copy-start | bytes 388
  7.2 44.6 %copy-start.5 = (u32[32]{0:T(128)S(1)}, u32[32]{0:T(128)}, u32[]{:S(2)}) copy-start(u32[32]{0:T(128)} %constant.68) | copy-start | bytes 388
  7.2 39.7 %copy-start.1 = (bf16[4,128,128]{2,1,0:T(8,128)(2,1)S(1)}, bf16[4,128,128]{2,1,0:T(8,128)(2,1)}, u32[]{:S(2)}) copy-start(bf16[4,128,128]{2,1,0:T(8,128)(2,1)} %param.12) | copy-start | bytes 393220
  7.2 330.1 %all-reduce.6.cloned.1.call-start = ((), (), s32[]{:S(2)}) async-start(), calls=%async_computation | async-start | bytes 5767168 | tf_op jit(solution)/shard_map/psum | solution.py:208
  34.6 3.9 %collective-permute-start = (bf16[1,8,128]{2,1,0:T(8,128)(2,1)S(1)}, bf16[1,8,128]{2,1,0:T(8,128)(2,1)S(1)}, u32[]{:S(2)}, u32[]{:S(2)}) collective-permute-start(bf16[1,8,128]{2,1,0:T(8,128)(2,1)S(1)} %get-tuple-element.71), channel_id=1, source_target_pairs={{0,4},{4,8},{8,12},{1,5},{5,9},{9,13},{2,6},{6,10},{10,14},{3,7},{... | collective-permute-start | bytes 6152 | tf_op jit(solution)/shard_map/ppermute | solution.py:21
  35.9 5.5 %collective-permute-start.1 = (bf16[1,8,128]{2,1,0:T(8,128)(2,1)S(1)}, bf16[1,8,128]{2,1,0:T(8,128)(2,1)S(1)}, u32[]{:S(2)}, u32[]{:S(2)}) collective-permute-start(bf16[1,8,128]{2,1,0:T(8,128)(2,1)S(1)} %get-tuple-element.72), channel_id=1, source_target_pairs={{4,0},{8,4},{12,8},{5,1},{9,5},{13,9},{6,2},{10,6},{14,10},{7,3},{... | collective-permute-start | bytes 6152 | tf_op jit(solution)/shard_map/ppermute | solution.py:22
  41.4 2.7 collective-permute-start.2
  42.7 3.1 collective-permute-start.3
  46.7 48.2 %copy-start.3 = (bf16[8,8,128]{2,1,0:T(8,128)(2,1)S(1)}, bf16[8,8,128]{2,1,0:T(8,128)(2,1)}, u32[]{:S(2)}) copy-start(bf16[8,8,128]{2,1,0:T(8,128)(2,1)} %param.13) | copy-start | bytes 49156
  47.4 6.6 %collective-permute-start.4 = (bf16[2,8,128]{2,1,0:T(8,128)(2,1)S(1)}, bf16[2,8,128]{2,1,0:T(8,128)(2,1)S(1)}, u32[]{:S(2)}, u32[]{:S(2)}) collective-permute-start(bf16[2,8,128]{2,1,0:T(8,128)(2,1)S(1)} %get-tuple-element.69), channel_id=1, source_target_pairs={{0,4},{4,8},{8,12},{1,5},{5,9},{9,13},{2,6},{6,10},{10,14},{3,7},{... | collective-permute-start | bytes 12296 | tf_op jit(solution)/shard_map/ppermute | solution.py:21
  49.7 5.5 %collective-permute-start.5 = (bf16[2,8,128]{2,1,0:T(8,128)(2,1)S(1)}, bf16[2,8,128]{2,1,0:T(8,128)(2,1)S(1)}, u32[]{:S(2)}, u32[]{:S(2)}) collective-permute-start(bf16[2,8,128]{2,1,0:T(8,128)(2,1)S(1)} %get-tuple-element.70), channel_id=1, source_target_pairs={{4,0},{8,4},{12,8},{5,1},{9,5},{13,9},{6,2},{10,6},{14,10},{7,3},{... | collective-permute-start | bytes 12296 | tf_op jit(solution)/shard_map/ppermute | solution.py:22
  55.3 4.1 %collective-permute-start.6 = (bf16[12,2,128]{2,1,0:T(2,128)(2,1)S(1)}, bf16[12,2,128]{2,1,0:T(2,128)(2,1)S(1)}, u32[]{:S(2)}, u32[]{:S(2)}) collective-permute-start(bf16[12,2,128]{2,1,0:T(2,128)(2,1)S(1)} %get-tuple-element.51), channel_id=1, source_target_pairs={{0,1},{1,2},{2,3},{4,5},{5,6},{6,7},{8,9},{9,10},{10,11},{12,13},{... | collective-permute-start | bytes 18440 | tf_op jit(solution)/shard_map/ppermute | solution.py:21
  57.9 3.8 %collective-permute-start.7 = (bf16[12,2,128]{2,1,0:T(2,128)(2,1)S(1)}, bf16[12,2,128]{2,1,0:T(2,128)(2,1)S(1)}, u32[]{:S(2)}, u32[]{:S(2)}) collective-permute-start(bf16[12,2,128]{2,1,0:T(2,128)(2,1)S(1)} %get-tuple-element.52), channel_id=1, source_target_pairs={{1,0},{2,1},{3,2},{5,4},{6,5},{7,6},{9,8},{10,9},{11,10},{13,12},{... | collective-permute-start | bytes 18440 | tf_op jit(solution)/shard_map/ppermute | solution.py:22
  63.3 5.3 %collective-permute-start.8 = (bf16[4,8,128]{2,1,0:T(8,128)(2,1)S(1)}, bf16[4,8,128]{2,1,0:T(8,128)(2,1)S(1)}, u32[]{:S(2)}, u32[]{:S(2)}) collective-permute-start(bf16[4,8,128]{2,1,0:T(8,128)(2,1)S(1)} %get-tuple-element.67), channel_id=1, source_target_pairs={{0,4},{4,8},{8,12},{1,5},{5,9},{9,13},{2,6},{6,10},{10,14},{3,7},{... | collective-permute-start | bytes 24584 | tf_op jit(solution)/shard_map/ppermute | solution.py:21
  67.2 5.5 %collective-permute-start.9 = (bf16[4,8,128]{2,1,0:T(8,128)(2,1)S(1)}, bf16[4,8,128]{2,1,0:T(8,128)(2,1)S(1)}, u32[]{:S(2)}, u32[]{:S(2)}) collective-permute-start(bf16[4,8,128]{2,1,0:T(8,128)(2,1)S(1)} %get-tuple-element.68), channel_id=1, source_target_pairs={{4,0},{8,4},{12,8},{5,1},{9,5},{13,9},{6,2},{10,6},{14,10},{7,3},{... | collective-permute-start | bytes 24584 | tf_op jit(solution)/shard_map/ppermute | solution.py:22
  72.8 7.2 %collective-permute-start.10 = (bf16[16,4,128]{2,1,0:T(4,128)(2,1)S(1)}, bf16[16,4,128]{2,1,0:T(4,128)(2,1)S(1)}, u32[]{:S(2)}, u32[]{:S(2)}) collective-permute-start(bf16[16,4,128]{2,1,0:T(4,128)(2,1)S(1)} %get-tuple-element.43), channel_id=1, source_target_pairs={{0,1},{1,2},{2,3},{4,5},{5,6},{6,7},{8,9},{9,10},{10,11},{12,13},{... | collective-permute-start | bytes 49160 | tf_op jit(solution)/shard_map/ppermute | solution.py:21
  75.6 4.1 %collective-permute-start.11 = (bf16[16,4,128]{2,1,0:T(4,128)(2,1)S(1)}, bf16[16,4,128]{2,1,0:T(4,128)(2,1)S(1)}, u32[]{:S(2)}, u32[]{:S(2)}) collective-permute-start(bf16[16,4,128]{2,1,0:T(4,128)(2,1)S(1)} %get-tuple-element.44), channel_id=1, source_target_pairs={{1,0},{2,1},{3,2},{5,4},{6,5},{7,6},{9,8},{10,9},{11,10},{13,12},{... | collective-permute-start | bytes 49160 | tf_op jit(solution)/shard_map/ppermute | solution.py:22
  81.0 6.0 %collective-permute-start.13 = (bf16[8,8,128]{2,1,0:T(8,128)(2,1)S(1)}, bf16[8,8,128]{2,1,0:T(8,128)(2,1)S(1)}, u32[]{:S(2)}, u32[]{:S(2)}) collective-permute-start(bf16[8,8,128]{2,1,0:T(8,128)(2,1)S(1)} %fusion.106), channel_id=1, source_target_pairs={{4,0},{8,4},{12,8},{5,1},{9,5},{13,9},{6,2},{10,6},{14,10},{7,3},{... | collective-permute-start | bytes 49160 | tf_op jit(solution)/shard_map/ppermute | solution.py:22
  82.3 6.0 %collective-permute-start.12 = (bf16[8,8,128]{2,1,0:T(8,128)(2,1)S(1)}, bf16[8,8,128]{2,1,0:T(8,128)(2,1)S(1)}, u32[]{:S(2)}, u32[]{:S(2)}) collective-permute-start(bf16[8,8,128]{2,1,0:T(8,128)(2,1)S(1)} %fusion.106), channel_id=1, source_target_pairs={{0,4},{4,8},{8,12},{1,5},{5,9},{9,13},{2,6},{6,10},{10,14},{3,7},{... | collective-permute-start | bytes 49160 | tf_op jit(solution)/shard_map/ppermute | solution.py:21
  88.3 5.4 %collective-permute-start.15 = (bf16[24,8,128]{2,1,0:T(8,128)(2,1)S(1)}, bf16[24,8,128]{2,1,0:T(8,128)(2,1)S(1)}, u32[]{:S(2)}, u32[]{:S(2)}) collective-permute-start(bf16[24,8,128]{2,1,0:T(8,128)(2,1)S(1)} %pad_maximum_fusion.3), channel_id=1, source_target_pairs={{1,0},{2,1},{3,2},{5,4},{6,5},{7,6},{9,8},{10,9},{11,10},{13,12},{... | collective-permute-start | bytes 147464 | tf_op jit(solution)/shard_map/ppermute | solution.py:22
  89.6 4.7 %collective-permute-start.14 = (bf16[24,8,128]{2,1,0:T(8,128)(2,1)S(1)}, bf16[24,8,128]{2,1,0:T(8,128)(2,1)S(1)}, u32[]{:S(2)}, u32[]{:S(2)}) collective-permute-start(bf16[24,8,128]{2,1,0:T(8,128)(2,1)S(1)} %pad_maximum_fusion.3), channel_id=1, source_target_pairs={{0,1},{1,2},{2,3},{4,5},{5,6},{6,7},{8,9},{9,10},{10,11},{12,13},{... | collective-permute-start | bytes 147464 | tf_op jit(solution)/shard_map/ppermute | solution.py:21
  95.1 8.3 %collective-permute-start.17 = (bf16[8,8,128]{2,1,0:T(8,128)(2,1)S(1)}, bf16[8,8,128]{2,1,0:T(8,128)(2,1)S(1)}, u32[]{:S(2)}, u32[]{:S(2)}) collective-permute-start(bf16[8,8,128]{2,1,0:T(8,128)(2,1)S(1)} %fusion.50), channel_id=1, source_target_pairs={{4,0},{8,4},{12,8},{5,1},{9,5},{13,9},{6,2},{10,6},{14,10},{7,3},{... | collective-permute-start | bytes 49160 | tf_op jit(solution)/shard_map/ppermute | solution.py:22
  96.4 7.0 %collective-permute-start.16 = (bf16[8,8,128]{2,1,0:T(8,128)(2,1)S(1)}, bf16[8,8,128]{2,1,0:T(8,128)(2,1)S(1)}, u32[]{:S(2)}, u32[]{:S(2)}) collective-permute-start(bf16[8,8,128]{2,1,0:T(8,128)(2,1)S(1)} %fusion.50), channel_id=1, source_target_pairs={{0,4},{4,8},{8,12},{1,5},{5,9},{9,13},{2,6},{6,10},{10,14},{3,7},{... | collective-permute-start | bytes 49160 | tf_op jit(solution)/shard_map/ppermute | solution.py:21
  103.4 5.2 %collective-permute-start.19 = (bf16[24,8,128]{2,1,0:T(8,128)(2,1)S(1)}, bf16[24,8,128]{2,1,0:T(8,128)(2,1)S(1)}, u32[]{:S(2)}, u32[]{:S(2)}) collective-permute-start(bf16[24,8,128]{2,1,0:T(8,128)(2,1)S(1)} %pad_maximum_fusion.4), channel_id=1, source_target_pairs={{0,1},{1,2},{2,3},{4,5},{5,6},{6,7},{8,9},{9,10},{10,11},{12,13},{... | collective-permute-start | bytes 147464 | tf_op jit(solution)/shard_map/ppermute | solution.py:21
  107.1 5.3 %collective-permute-start.18 = (bf16[24,8,128]{2,1,0:T(8,128)(2,1)S(1)}, bf16[24,8,128]{2,1,0:T(8,128)(2,1)S(1)}, u32[]{:S(2)}, u32[]{:S(2)}) collective-permute-start(bf16[24,8,128]{2,1,0:T(8,128)(2,1)S(1)} %pad_maximum_fusion.4), channel_id=1, source_target_pairs={{1,0},{2,1},{3,2},{5,4},{6,5},{7,6},{9,8},{10,9},{11,10},{13,12},{... | collective-permute-start | bytes 147464 | tf_op jit(solution)/shard_map/ppermute | solution.py:22
  113.7 7.3 %collective-permute-start.20 = (bf16[4,8,128]{2,1,0:T(8,128)(2,1)S(1)}, bf16[4,8,128]{2,1,0:T(8,128)(2,1)S(1)}, u32[]{:S(2)}, u32[]{:S(2)}) collective-permute-start(bf16[4,8,128]{2,1,0:T(8,128)(2,1)S(1)} %get-tuple-element.65), channel_id=1, source_target_pairs={{0,4},{4,8},{8,12},{1,5},{5,9},{9,13},{2,6},{6,10},{10,14},{3,7},{... | collective-permute-start | bytes 24584 | tf_op jit(solution)/shard_map/ppermute | solution.py:21
  117.7 5.5 %collective-permute-start.21 = (bf16[4,8,128]{2,1,0:T(8,128)(2,1)S(1)}, bf16[4,8,128]{2,1,0:T(8,128)(2,1)S(1)}, u32[]{:S(2)}, u32[]{:S(2)}) collective-permute-start(bf16[4,8,128]{2,1,0:T(8,128)(2,1)S(1)} %get-tuple-element.66), channel_id=1, source_target_pairs={{4,0},{8,4},{12,8},{5,1},{9,5},{13,9},{6,2},{10,6},{14,10},{7,3},{... | collective-permute-start | bytes 24584 | tf_op jit(solution)/shard_map/ppermute | solution.py:22
  123.2 6.3 %collective-permute-start.22 = (bf16[16,4,128]{2,1,0:T(4,128)(2,1)S(1)}, bf16[16,4,128]{2,1,0:T(4,128)(2,1)S(1)}, u32[]{:S(2)}, u32[]{:S(2)}) collective-permute-start(bf16[16,4,128]{2,1,0:T(4,128)(2,1)S(1)} %get-tuple-element.41), channel_id=1, source_target_pairs={{1,0},{2,1},{3,2},{5,4},{6,5},{7,6},{9,8},{10,9},{11,10},{13,12},{... | collective-permute-start | bytes 49160 | tf_op jit(solution)/shard_map/ppermute | solution.py:22
  124.5 4.7 %collective-permute-start.23 = (bf16[16,4,128]{2,1,0:T(4,128)(2,1)S(1)}, bf16[16,4,128]{2,1,0:T(4,128)(2,1)S(1)}, u32[]{:S(2)}, u32[]{:S(2)}) collective-permute-start(bf16[16,4,128]{2,1,0:T(4,128)(2,1)S(1)} %get-tuple-element.42), channel_id=1, source_target_pairs={{0,1},{1,2},{2,3},{4,5},{5,6},{6,7},{8,9},{9,10},{10,11},{12,13},{... | collective-permute-start | bytes 49160 | tf_op jit(solution)/shard_map/ppermute | solution.py:21
  132.1 5.4 %collective-permute-start.24 = (bf16[2,8,128]{2,1,0:T(8,128)(2,1)S(1)}, bf16[2,8,128]{2,1,0:T(8,128)(2,1)S(1)}, u32[]{:S(2)}, u32[]{:S(2)}) collective-permute-start(bf16[2,8,128]{2,1,0:T(8,128)(2,1)S(1)} %get-tuple-element.63), channel_id=1, source_target_pairs={{0,4},{4,8},{8,12},{1,5},{5,9},{9,13},{2,6},{6,10},{10,14},{3,7},{... | collective-permute-start | bytes 12296 | tf_op jit(solution)/shard_map/ppermute | solution.py:21
  135.4 5.5 %collective-permute-start.25 = (bf16[2,8,128]{2,1,0:T(8,128)(2,1)S(1)}, bf16[2,8,128]{2,1,0:T(8,128)(2,1)S(1)}, u32[]{:S(2)}, u32[]{:S(2)}) collective-permute-start(bf16[2,8,128]{2,1,0:T(8,128)(2,1)S(1)} %get-tuple-element.64), channel_id=1, source_target_pairs={{4,0},{8,4},{12,8},{5,1},{9,5},{13,9},{6,2},{10,6},{14,10},{7,3},{... | collective-permute-start | bytes 12296 | tf_op jit(solution)/shard_map/ppermute | solution.py:22
  140.9 4.5 %collective-permute-start.26 = (bf16[12,2,128]{2,1,0:T(2,128)(2,1)S(1)}, bf16[12,2,128]{2,1,0:T(2,128)(2,1)S(1)}, u32[]{:S(2)}, u32[]{:S(2)}) collective-permute-start(bf16[12,2,128]{2,1,0:T(2,128)(2,1)S(1)} %get-tuple-element.47), channel_id=1, source_target_pairs={{1,0},{2,1},{3,2},{5,4},{6,5},{7,6},{9,8},{10,9},{11,10},{13,12},{... | collective-permute-start | bytes 18440 | tf_op jit(solution)/shard_map/ppermute | solution.py:22
  142.2 3.8 %collective-permute-start.27 = (bf16[12,2,128]{2,1,0:T(2,128)(2,1)S(1)}, bf16[12,2,128]{2,1,0:T(2,128)(2,1)S(1)}, u32[]{:S(2)}, u32[]{:S(2)}) collective-permute-start(bf16[12,2,128]{2,1,0:T(2,128)(2,1)S(1)} %get-tuple-element.48), channel_id=1, source_target_pairs={{0,1},{1,2},{2,3},{4,5},{5,6},{6,7},{8,9},{9,10},{10,11},{12,13},{... | collective-permute-start | bytes 18440 | tf_op jit(solution)/shard_map/ppermute | solution.py:21
  149.5 7.4 %collective-permute-start.28 = (bf16[1,8,128]{2,1,0:T(8,128)(2,1)S(1)}, bf16[1,8,128]{2,1,0:T(8,128)(2,1)S(1)}, u32[]{:S(2)}, u32[]{:S(2)}) collective-permute-start(bf16[1,8,128]{2,1,0:T(8,128)(2,1)S(1)} %get-tuple-element.61), channel_id=1, source_target_pairs={{0,4},{4,8},{8,12},{1,5},{5,9},{9,13},{2,6},{6,10},{10,14},{3,7},{... | collective-permute-start | bytes 6152 | tf_op jit(solution)/shard_map/ppermute | solution.py:21
  152.8 5.5 %collective-permute-start.29 = (bf16[1,8,128]{2,1,0:T(8,128)(2,1)S(1)}, bf16[1,8,128]{2,1,0:T(8,128)(2,1)S(1)}, u32[]{:S(2)}, u32[]{:S(2)}) collective-permute-start(bf16[1,8,128]{2,1,0:T(8,128)(2,1)S(1)} %get-tuple-element.62), channel_id=1, source_target_pairs={{4,0},{8,4},{12,8},{5,1},{9,5},{13,9},{6,2},{10,6},{14,10},{7,3},{... | collective-permute-start | bytes 6152 | tf_op jit(solution)/shard_map/ppermute | solution.py:22
  154.6 81.4 %copy-start.4 = (bf16[2,256]{1,0:T(2,128)(2,1)S(1)}, bf16[2,256]{1,0:T(2,128)(2,1)}, u32[]{:S(2)}) copy-start(bf16[2,256]{1,0:T(2,128)(2,1)} %param.7) | copy-start | bytes 3076
  158.3 6.1 %collective-permute-start.30 = (bf16[10,1,128]{2,1,0:T(2,128)(2,1)S(1)}, bf16[10,1,128]{2,1,0:T(2,128)(2,1)S(1)}, u32[]{:S(2)}, u32[]{:S(2)}) collective-permute-start(bf16[10,1,128]{2,1,0:T(2,128)(2,1)S(1)} %get-tuple-element.55), channel_id=1, source_target_pairs={{1,0},{2,1},{3,2},{5,4},{6,5},{7,6},{9,8},{10,9},{11,10},{13,12},{... | collective-permute-start | bytes 7688 | tf_op jit(solution)/shard_map/ppermute | solution.py:22
  159.6 5.4 %collective-permute-start.31 = (bf16[10,1,128]{2,1,0:T(2,128)(2,1)S(1)}, bf16[10,1,128]{2,1,0:T(2,128)(2,1)S(1)}, u32[]{:S(2)}, u32[]{:S(2)}) collective-permute-start(bf16[10,1,128]{2,1,0:T(2,128)(2,1)S(1)} %get-tuple-element.56), channel_id=1, source_target_pairs={{0,1},{1,2},{2,3},{4,5},{5,6},{6,7},{8,9},{9,10},{10,11},{12,13},{... | collective-permute-start | bytes 7688 | tf_op jit(solution)/shard_map/ppermute | solution.py:21
  165.5 72.5 %copy-start = (bf16[2,256,128]{2,1,0:T(8,128)(2,1)S(1)}, bf16[2,256,128]{2,1,0:T(8,128)(2,1)}, u32[]{:S(2)}) copy-start(bf16[2,256,128]{2,1,0:T(8,128)(2,1)} %param.9) | copy-start | bytes 393220
  339.1 3.4 copy-start.2
Sparse Core Ops, SparseCore 0:
  237.4 99.8 all-reduce.5
where the time goes:
time: 351 us; the launch traced here: 350 us
  waiting for transfers between devices  127 us (36%)
  blocking collectives  92.6 us (26%)
  starting transfers between devices  73.6 us (21%)
  matrix products  24.4 us (7%)
  between operations  16.3 us (5%)
  local copies, waits for them, and re-layouts  9.82 us (3%)
  other arithmetic  6.18 us (2%)
    psum x1, waiting for transfers between devices, body(): lax.psum((gain_grad, conv_grad, proj_grad, embed_term), ('row', 'col'))  98.4 us
    unnamed x2, blocking collectives  69.3 us
    ppermute x16, starting transfers between devices, with_halo(): before = lax.ppermute(last, axis, up)  52.9 us
    ppermute x16, waiting for transfers between devices, with_halo(): after = lax.ppermute(first, axis, down)  25 us
    all_gather x1, blocking collectives, body(): gathered = lax.all_gather(seq_feat, ('row', 'col'), axis=0, tiled=True)  23.3 us
    ppermute x16, starting transfers between devices, with_halo(): after = lax.ppermute(first, axis, down)  20.7 us
    dot_general x36, matrix products, conv_weight_grad(): lax.dot_general(window.reshape(height * width, channels), flat_grad, (((0...  7.69 us
    unnamed x20, local copies, waits for them, and re-layouts  7.07 us
  transfers between devices with their start and end apart: 33, of which 16 were waited for; matrix products, arithmetic and copies ran while one was open for 4% of the time, Pallas kernels for 0%

commit v1 on v0

--- a/solution.py
+++ b/solution.py
@@ -1,8 +1,11 @@
+import functools
 import math
 
 import jax
 import jax.numpy as jnp
 from jax import lax
+from jax.experimental import pallas as pl
+from jax.experimental.pallas import tpu as pltpu
 from jax.sharding import PartitionSpec as P
 
 LAYERS = 4
@@ -95,7 +98,7 @@
     return jnp.stack(terms)
 
 
-def body(seq_feat, lengths, embed_weight, norm_gain, conv_weight, proj_weight, pair_cotangent):
+def tiled_body(seq_feat, lengths, embed_weight, norm_gain, conv_weight, proj_weight, pair_cotangent):
     tile_rows = pair_cotangent.shape[0]
     tile_cols = pair_cotangent.shape[1]
     channels = pair_cotangent.shape[2]
@@ -211,6 +214,317 @@
     return (pair_output, seq_grad, embed_grad, gain_grad, conv_grad, proj_grad)
 
 
+NT = (((1,), (1,)), ((), ()))
+TN = (((0,), (0,)), ((), ()))
+NN = (((1,), (0,)), ((), ()))
+
+
+def dot(a, b, dims):
+    return lax.dot_general(a, b, dims, preferred_element_type=jnp.float32)
+
+
+def most_live(residues):
+    return residues - residues // 4
+
+
+def block_kernel(
+    grid_rows,
+    grid_cols,
+    lengths_ref,
+    *refs,
+):
+    pieces, (embed_ref, gain_ref, conv_hbm, proj_ref) = refs[:4], refs[4:8]
+    (pair_ref, seq_grad_ref, embed_grad_ref, gain_grad_ref, conv_grad_hbm, proj_grad_ref) = refs[8:14]
+    (
+        weights,
+        weight_sem,
+        stream,
+        back,
+        live,
+        shifted,
+        taps,
+        normed,
+        inv,
+        slope,
+        squashed,
+        conv_slope,
+        excited,
+        masked,
+        spread,
+        seq_lo,
+        seq_hi,
+        conv_grad,
+        grad_sem,
+    ) = refs[14:]
+    tile_rows, tile_cols, channels = pair_ref.shape
+    residues = tile_rows * grid_rows
+    own = seq_grad_ref.shape[0]
+    height = most_live(residues)
+    pitch = residues
+    count = height * pitch
+    margin = 2 ** (LAYERS - 1)
+    pad = margin * pitch
+    chunk_rows = 8
+    chunk = chunk_rows * pitch
+    chunks = [slice(k * chunk, (k + 1) * chunk) for k in range(height // chunk_rows)]
+    row, col = lax.axis_index("row"), lax.axis_index("col")
+    live_count = lengths_ref[0]
+
+    loads = [
+        pltpu.make_async_copy(conv_hbm.at[k], weights.at[k], weight_sem.at[k])
+        for k in range(LAYERS)
+    ]
+    for load in loads:
+        load.start()
+
+    piece_rows = pieces[0].shape[0] // grid_rows
+    tile = tile_rows * tile_cols
+    half = seq_lo.shape[1]
+    for step_col in range(grid_cols):
+        source_col = lax.rem(col + grid_cols - step_col, grid_cols)
+        for step_row in range(grid_rows):
+            source_row = lax.rem(row + grid_rows - step_row, grid_rows)
+            piece = pieces[step_col][step_row * piece_rows : (step_row + 1) * piece_rows, :].astype(
+                jnp.float32
+            )
+            back[
+                pl.ds(pl.multiple_of(source_row * tile_rows, tile_rows), tile_rows),
+                pl.ds(pl.multiple_of(source_col * tile_cols, tile_cols), tile_cols),
+                :,
+            ] = piece[:tile].reshape(tile_rows, tile_cols, channels)
+            owner = source_row * grid_cols + source_col
+            spread[pl.ds(pl.multiple_of(owner * 8, 8), 8), :] = piece[tile : tile + 8]
+    owners = grid_rows * grid_cols
+    for k in range(own):
+        seq_lo[pl.ds(k, owners, stride=own), :] = spread[pl.ds(k, owners, stride=8), :]
+        seq_hi[pl.ds(k, owners, stride=own), :] = spread[pl.ds(own + k, owners, stride=8), :]
+    seq = jnp.concatenate([seq_lo[...], seq_hi[...]], axis=1).astype(jnp.bfloat16)
+
+    pixel = lax.broadcasted_iota(jnp.int32, (residues, pitch, channels), 0)
+    pixel = jnp.maximum(pixel, lax.broadcasted_iota(jnp.int32, (residues, pitch, channels), 1))
+    live[...] = (pixel < live_count).astype(jnp.float32)
+
+    shifted[...] = jnp.zeros_like(shifted)
+    taps[...] = jnp.zeros_like(taps)
+
+    row_emb = dot(seq, embed_ref[0], NN).astype(jnp.bfloat16).astype(jnp.float32)
+    col_emb = dot(seq, embed_ref[1], NN).astype(jnp.bfloat16).astype(jnp.float32)
+    stream[...] = live[...] * (row_emb[:, None, :] + col_emb[None, :, :])
+
+    flat = lambda ref: ref.reshape(residues * pitch, channels)
+    stream_flat, live_flat, back_flat = flat(stream), flat(live), flat(back)
+
+    def lane_mean(x):
+        return jnp.mean(x, axis=-1, keepdims=True)
+
+    def window(part, spacing, direction):
+        return jnp.concatenate(
+            [
+                taps[
+                    pad + part.start + direction * a * spacing * pitch : pad
+                    + part.stop
+                    + direction * a * spacing * pitch,
+                    :,
+                ]
+                for a in (-1, 0, 1)
+            ],
+            axis=1,
+        )
+
+    def fill_taps(part, spacing, direction):
+        for b in (-1, 0, 1):
+            start = margin + part.start + direction * b * spacing
+            taps[pad + part.start : pad + part.stop, (b + 1) * channels : (b + 2) * channels] = (
+                shifted[start : start + chunk, :].astype(jnp.bfloat16)
+            )
+
+    for layer in range(LAYERS):
+        spacing = 2**layer
+        gain = gain_ref[layer : layer + 1, :]
+        for part in chunks:
+            value = stream_flat[part, :]
+            centred = value - lane_mean(value)
+            inv_std = lax.rsqrt(lane_mean(centred * centred) + eps)
+            normalized = centred * inv_std
+            scaled = normalized * gain
+            decay = jnp.exp(jnp.minimum(scaled, 0.0))
+            activated = jnp.maximum(scaled, 0.0) + (decay - 1.0)
+            normed[layer, part, :] = normalized
+            inv[layer, part, :] = jnp.broadcast_to(inv_std, normalized.shape)
+            slope[layer, part, :] = decay * live_flat[part, :]
+            shifted[margin + part.start : margin + part.stop, :] = activated
+            squashed[layer, part, :] = activated.astype(jnp.bfloat16)
+        for part in chunks:
+            fill_taps(part, spacing, 1)
+        loads[layer].wait()
+        for part in chunks:
+            convolved = dot(window(part, spacing, 1), weights[layer], NN)
+            decay = jnp.exp(jnp.minimum(convolved, 0.0))
+            conv_slope[layer, part, :] = decay
+            hidden = (jnp.maximum(convolved, 0.0) + (decay - 1.0)).astype(jnp.bfloat16)
+            excited[layer, part, :] = hidden
+            update = dot(hidden, proj_ref[layer], NN)
+            stream_flat[part, :] = stream_flat[part, :] + live_flat[part, :] * update
+
+    pair_ref[...] = stream[
+        pl.ds(pl.multiple_of(row * tile_rows, tile_rows), tile_rows),
+        pl.ds(pl.multiple_of(col * tile_cols, tile_cols), tile_cols),
+        :,
+    ].astype(jnp.bfloat16)
+
+    grad_scale = 1.0 / residues
+    for part in chunks:
+        back_flat[part, :] = back_flat[part, :] * live_flat[part, :]
+    stores = []
+    for layer in reversed(range(LAYERS)):
+        spacing = 2**layer
+        gain = gain_ref[layer : layer + 1, :]
+        for part in chunks:
+            grad = back_flat[part, :].astype(jnp.bfloat16)
+            masked[part, :] = grad
+            shifted[margin + part.start : margin + part.stop, :] = (
+                dot(grad, proj_ref[layer], NT) * conv_slope[layer, part, :]
+            )
+        for part in chunks:
+            fill_taps(part, spacing, -1)
+        proj_grad_ref[layer] = dot(excited[layer], masked[...], TN) * grad_scale
+        back_weights = jnp.concatenate(
+            [weights[layer, t * channels : (t + 1) * channels, :] for t in range(9)], axis=1
+        )
+        gain_total = jnp.zeros((1, channels), jnp.float32)
+        for part in chunks:
+            d_squashed = dot(window(part, spacing, -1), back_weights, NT)
+            normalized = normed[layer, part, :]
+            d_scaled = d_squashed * slope[layer, part, :]
+            gain_total = gain_total + jnp.sum(d_scaled * normalized, axis=0, keepdims=True)
+            d_norm = d_scaled * gain
+            back_flat[part, :] = back_flat[part, :] + inv[layer, part, :] * (
+                d_norm - lane_mean(d_norm) - normalized * lane_mean(d_norm * normalized)
+            )
+        gain_grad_ref[layer : layer + 1, :] = gain_total * grad_scale
+        every = slice(0, count)
+        weight_grad = dot(squashed[layer], window(every, spacing, -1), TN) * grad_scale
+        for t in range(9):
+            conv_grad[layer, t] = weight_grad[:, t * channels : (t + 1) * channels]
+        store = pltpu.make_async_copy(
+            conv_grad.at[layer], conv_grad_hbm.at[layer], grad_sem.at[layer]
+        )
+        store.start()
+        stores.append(store)
+
+    final = back[...]
+    beyond = lax.broadcasted_iota(jnp.int32, (residues, pitch, channels), 0) < height
+    final = jnp.where(beyond, final, 0.0)
+    d_row = jnp.sum(final, axis=1).astype(jnp.bfloat16)
+    d_col = jnp.sum(final, axis=0).astype(jnp.bfloat16)
+    embed_grad_ref[0] = dot(seq, d_row, TN) * grad_scale
+    embed_grad_ref[1] = dot(seq, d_col, TN) * grad_scale
+    seq_grad = (dot(d_row, embed_ref[0], NT) + dot(d_col, embed_ref[1], NT)) / math.sqrt(residues)
+    first = own * (row * grid_cols + col)
+    for k in range(own):
+        chosen = lax.broadcasted_iota(jnp.int32, seq_grad.shape, 0) == first + k
+        seq_grad_ref[k : k + 1, :] = jnp.sum(
+            jnp.where(chosen, seq_grad, 0.0), axis=0, keepdims=True
+        )
+    for store in stores:
+        store.wait()
+
+
+def replicated_body(
+    seq_feat, lengths, embed_weight, norm_gain, conv_weight, proj_weight, pair_cotangent
+):
+    tile_rows, tile_cols, channels = pair_cotangent.shape
+    grid_rows, grid_cols = lax.axis_size("row"), lax.axis_size("col")
+    residues = tile_rows * grid_rows
+    height, pitch = most_live(residues), residues
+    margin = 2 ** (LAYERS - 1)
+    own, features = seq_feat.shape
+    halves = features // channels
+    seq_rows = jnp.concatenate(
+        [seq_feat[:, k * channels : (k + 1) * channels] for k in range(halves)], axis=0
+    )
+    payload = jnp.concatenate(
+        [
+            pair_cotangent.reshape(tile_rows * tile_cols, channels),
+            seq_rows,
+            jnp.zeros((16 - own * halves, channels), jnp.bfloat16),
+        ],
+        axis=0,
+    )
+
+    def rotate(x, axis, count, step):
+        return lax.ppermute(x, axis, [(i, (i + step) % count) for i in range(count)])
+
+    column = jnp.concatenate(
+        [payload] + [rotate(payload, "row", grid_rows, k) for k in range(1, grid_rows)], axis=0
+    )
+    pieces = [column] + [rotate(column, "col", grid_cols, k) for k in range(1, grid_cols)]
+    count = height * pitch
+    taps_rows = count + 2 * margin * pitch
+    f32, bf16 = jnp.float32, jnp.bfloat16
+    vmem = pl.BlockSpec(memory_space=pltpu.VMEM)
+    hbm = pl.BlockSpec(memory_space=pl.ANY)
+    outs = pl.pallas_call(
+        functools.partial(block_kernel, grid_rows, grid_cols),
+        out_shape=(
+            jax.ShapeDtypeStruct((tile_rows, tile_cols, channels), bf16),
+            jax.ShapeDtypeStruct((own, features), f32),
+            jax.ShapeDtypeStruct((2, features, channels), f32),
+            jax.ShapeDtypeStruct((LAYERS, channels), f32),
+            jax.ShapeDtypeStruct((LAYERS, 9, channels, channels), f32),
+            jax.ShapeDtypeStruct((LAYERS, channels, channels), f32),
+        ),
+        in_specs=[pl.BlockSpec(memory_space=pltpu.SMEM)] + [vmem] * 6 + [hbm, vmem],
+        out_specs=(vmem, vmem, vmem, vmem, hbm, vmem),
+        scratch_shapes=[
+            pltpu.VMEM((LAYERS, 9 * channels, channels), bf16),
+            pltpu.SemaphoreType.DMA((LAYERS,)),
+            pltpu.VMEM((residues, pitch, channels), f32),
+            pltpu.VMEM((residues, pitch, channels), f32),
+            pltpu.VMEM((residues, pitch, channels), f32),
+            pltpu.VMEM((count + 2 * margin, channels), f32),
+            pltpu.VMEM((taps_rows, 3 * channels), bf16),
+            pltpu.VMEM((LAYERS, count, channels), f32),
+            pltpu.VMEM((LAYERS, count, channels), f32),
+            pltpu.VMEM((LAYERS, count, channels), f32),
+            pltpu.VMEM((LAYERS, count, channels), bf16),
+            pltpu.VMEM((LAYERS, count, channels), f32),
+            pltpu.VMEM((LAYERS, count, channels), bf16),
+            pltpu.VMEM((count, channels), bf16),
+            pltpu.VMEM((8 * grid_rows * grid_cols, channels), f32),
+            pltpu.VMEM((residues, channels), f32),
+            pltpu.VMEM((residues, channels), f32),
+            pltpu.VMEM((LAYERS, 9, channels, channels), f32),
+            pltpu.SemaphoreType.DMA((LAYERS,)),
+        ],
+        compiler_params=pltpu.CompilerParams(vmem_limit_bytes=48 * 1024 * 1024),
+    )(
+        lengths,
+        *pieces,
+        embed_weight,
+        norm_gain,
+        conv_weight.reshape(LAYERS, 9 * channels, channels),
+        proj_weight,
+    )
+    pair_output, seq_grad, embed_grad, gain_grad, conv_grad, proj_grad = outs
+    return (
+        pair_output,
+        seq_grad,
+        embed_grad,
+        gain_grad,
+        conv_grad.reshape(LAYERS, 3, 3, channels, channels),
+        proj_grad,
+    )
+
+
+def body(seq_feat, lengths, embed_weight, norm_gain, conv_weight, proj_weight, pair_cotangent):
+    residues = pair_cotangent.shape[0] * lax.axis_size("row")
+    plan = replicated_body if residues <= 32 else tiled_body
+    return plan(
+        seq_feat, lengths, embed_weight, norm_gain, conv_weight, proj_weight, pair_cotangent
+    )
+
+
 def solution(mesh):
     placed = (
         P(("groups", "row", "col"), None),

time: 351 us -> 36.7 us (0.10)
  waiting for transfers between devices: 127 us -> 9.38 us
  blocking collectives: 92.6 us -> 0 us
  starting transfers between devices: 73.6 us -> 7.83 us
  matrix products: 24.4 us -> 0 us
  between operations: 16.3 us -> 0.65 us
  Pallas kernels: 0 us -> 11.7 us
  other arithmetic: 6.18 us -> 0.73 us
  local copies, waits for them, and re-layouts: 9.82 us -> 5.98 us
    psum x1 -> x0, waiting for transfers between devices: 98.4 us -> none  [body(): lax.psum((gain_grad, conv_grad, proj_grad, embed_term), ('row', 'col'))]
    unnamed x2 -> x0, blocking collectives: 69.3 us -> none
    ppermute x32 -> x6, starting transfers between devices: 73.6 us -> 7.83 us  [rotate(): lax.ppermute(x, axis, [(i, (i + step) % count) for i in range(count)])]
    dot_general x126 -> x0, matrix products: 24.4 us -> none  [the longest x36 7.69 us: conv_weight_grad(): lax.dot_general(window.reshape(height * width, channels), flat_grad, (((0...]
    all_gather x1 -> x0, blocking collectives: 23.3 us -> none  [body(): gathered = lax.all_gather(seq_feat, ('row', 'col'), axis=0, tiled=True)]
    ppermute x32 -> x6, waiting for transfers between devices: 28.6 us -> 9.38 us  [rotate(): lax.ppermute(x, axis, [(i, (i + step) % count) for i in range(count)])]
    pallas_call x0 -> x1, Pallas kernels: none -> 11.7 us  [replicated_body(): pl.pallas_call(functools.partial(block_kernel, grid_rows, grid_cols), out...]
    unnamed x20 -> x10, local copies, waits for them, and re-layouts: 7.07 us -> 4.41 us
  transfers between devices with their start and end apart: 33 -> 6, of which waited for: 16 -> 6; matrix products, arithmetic and copies ran while one was open for 4% -> 0% of each run, Pallas kernels for 0% -> 0%
where the time goes in v1:
time: 36.7 us; the launch traced here: 36.3 us
  Pallas kernels  11.7 us (32%)
  waiting for transfers between devices  9.38 us (26%)
  starting transfers between devices  7.83 us (21%)
  local copies, waits for them, and re-layouts  5.98 us (16%)
  other arithmetic  0.73 us (2%)
  between operations  0.65 us (2%)
    pallas_call x1, Pallas kernels, replicated_body(): pl.pallas_call(functools.partial(block_kernel, grid_rows, grid_cols), out...  11.7 us
    ppermute x6, waiting for transfers between devices, rotate(): lax.ppermute(x, axis, [(i, (i + step) % count) for i in range(count)])  9.38 us
    ppermute x6, starting transfers between devices, rotate(): lax.ppermute(x, axis, [(i, (i + step) % count) for i in range(count)])  7.83 us
    unnamed x10, local copies, waits for them, and re-layouts  4.41 us
    concatenate x1, local copies, waits for them, and re-layouts, replicated_body(): jnp.concatenate([payload] + [rotate(payload, 'row', grid_rows, k) for k i...  0.88 us
  transfers between devices with their start and end apart: 6, of which 6 were waited for; matrix products, arithmetic and copies ran while one was open for 0% of the time, Pallas kernels for 0%

profile of v1, /device:TPU:0, one launch (start us, length us, event | category | flops | bytes accessed | tf_op | source)
XLA Modules:
  0.0 36.3 jit_solution(12024328774760545677)
XLA Ops:
  0.6 0.7 %fusion = (bf16[2,128]{1,0:T(2,128)(2,1)S(1)}, bf16[2,128]{1,0:T(2,128)(2,1)S(1)}) fusion(bf16[2,256]{1,0:T(2,128)(2,1)} %param.7), kind=kLoop, calls=%fused_computation.1 | loop fusion | bytes 2048 | tf_op jit(solution)/shard_map/slice | solution.py:444
  1.3 0.7 %pad_maximum_fusion = bf16[80,128]{1,0:T(8,128)(2,1)S(1)} fusion(bf16[12,128]{1,0:T(8,128)(2,1)S(1)} %broadcast_in_dim.3, bf16[2,128]{1,0:T(2,128)(2,1)S(1)} %get-tuple-element.18, bf16[2,128]{1,0:T(2,128)(2,1)S(1)} %get-tuple-element.19, bf16[64,128]{1,0:T(8,128)(2,1)} %bitcast.4), kind=kLoop, calls=%fused_computation | loop fusion | flops 81920 | bytes 40960 | tf_op jit(solution)/shard_map/concatenate | solution.py:446
  2.0 5.0 %collective-permute-start.2 = (bf16[80,128]{1,0:T(8,128)(2,1)S(1)}, bf16[80,128]{1,0:T(8,128)(2,1)S(1)}, u32[]{:S(2)}, u32[]{:S(2)}) collective-permute-start(bf16[80,128]{1,0:T(8,128)(2,1)S(1)} %pad_maximum_fusion), channel_id=1, source_target_pairs={{0,12},{4,0},{8,4},{12,8},{1,13},{5,1},{9,5},{13,9},{2,14},{6,2},{... | collective-permute-start | bytes 61448 | tf_op jit(solution)/shard_map/ppermute | solution.py:456
  7.1 0.0 collective-permute-start.1
  7.1 1.0 %collective-permute-start = (bf16[80,128]{1,0:T(8,128)(2,1)S(1)}, bf16[80,128]{1,0:T(8,128)(2,1)S(1)}, u32[]{:S(2)}, u32[]{:S(2)}) collective-permute-start(bf16[80,128]{1,0:T(8,128)(2,1)S(1)} %pad_maximum_fusion), channel_id=1, source_target_pairs={{0,4},{4,8},{8,12},{12,0},{1,5},{5,9},{9,13},{13,1},{2,6},{6,10},{... | collective-permute-start | bytes 61448 | tf_op jit(solution)/shard_map/ppermute | solution.py:456
  8.1 0.5 %collective-permute-done.2 = bf16[80,128]{1,0:T(8,128)(2,1)S(1)} collective-permute-done((bf16[80,128]{1,0:T(8,128)(2,1)S(1)}, bf16[80,128]{1,0:T(8,128)(2,1)S(1)}, u32[]{:S(2)}, u32[]{:S(2)}) %collective-permute-start.2) | collective-permute-done | bytes 20512 | tf_op jit(solution)/shard_map/ppermute | solution.py:456
  8.6 3.2 %collective-permute-done.1 = bf16[80,128]{1,0:T(8,128)(2,1)S(1)} collective-permute-done((bf16[80,128]{1,0:T(8,128)(2,1)S(1)}, bf16[80,128]{1,0:T(8,128)(2,1)S(1)}, u32[]{:S(2)}, u32[]{:S(2)}) %collective-permute-start.1) | collective-permute-done | bytes 20512 | tf_op jit(solution)/shard_map/ppermute | solution.py:456
  11.8 0.9 %collective-permute-done = bf16[80,128]{1,0:T(8,128)(2,1)S(1)} collective-permute-done((bf16[80,128]{1,0:T(8,128)(2,1)S(1)}, bf16[80,128]{1,0:T(8,128)(2,1)S(1)}, u32[]{:S(2)}, u32[]{:S(2)}) %collective-permute-start) | collective-permute-done | bytes 20512 | tf_op jit(solution)/shard_map/ppermute | solution.py:456
  12.7 0.9 %concatenate.8.refs_0_ = bf16[320,128]{1,0:T(8,128)(2,1)S(1)} concatenate(bf16[64,128]{1,0:T(8,128)(2,1)} %bitcast.5, bf16[2,128]{1,0:T(2,128)(2,1)S(1)} %get-tuple-element.19, bf16[2,128]{1,0:T(2,128)(2,1)S(1)} %get-tuple-element.18, bf16[12,128]{1,0:T(8,128)(2,1)S(1)} %broadcast_in_dim.3, bf16[80,128]{1,0:T(8,128)(2,1)S(1)} %collective-permute-done, ...), dimensions={0} | concatenate | bytes 163840 | tf_op jit(solution)/shard_map/concatenate | solution.py:458
  13.6 0.0 collective-permute-start.5
  13.6 1.6 %collective-permute-start.4 = (bf16[320,128]{1,0:T(8,128)(2,1)S(1)}, bf16[320,128]{1,0:T(8,128)(2,1)S(1)}, u32[]{:S(2)}, u32[]{:S(2)}) collective-permute-start(bf16[320,128]{1,0:T(8,128)(2,1)S(1)} %concatenate.8.refs_0_), channel_id=1, source_target_pairs={{0,2},{1,3},{2,0},{3,1},{4,6},{5,7},{6,4},{7,5},{8,10},{9,11},{10,... | collective-permute-start | bytes 245768 | tf_op jit(solution)/shard_map/ppermute | solution.py:456
  15.2 0.2 collective-permute-start.3
  15.3 0.3 collective-permute-done.5.refs_3_
  15.7 4.4 %collective-permute-done.4.refs_2_ = bf16[320,128]{1,0:T(8,128)(2,1)S(1)} collective-permute-done((bf16[320,128]{1,0:T(8,128)(2,1)S(1)}, bf16[320,128]{1,0:T(8,128)(2,1)S(1)}, u32[]{:S(2)}, u32[]{:S(2)}) %collective-permute-start.4) | collective-permute-done | bytes 81952 | tf_op jit(solution)/shard_map/ppermute | solution.py:456
  20.1 0.1 collective-permute-done.3.refs_1_
  20.1 0.0 copy-start
  20.1 1.3 %copy-done = bf16[4,3,3,128,128]{4,3,2,1,0:T(8,128)(2,1)S(1)} copy-done((bf16[4,3,3,128,128]{4,3,2,1,0:T(8,128)(2,1)S(1)}, bf16[4,3,3,128,128]{4,3,2,1,0:T(8,128)(2,1)}, u32[]{:S(2)}) %copy-start) | copy-done | bytes 1179672
  21.4 0.0 copy-start.1
  21.4 0.9 %copy-done.1 = bf16[2,256,128]{2,1,0:T(8,128)(2,1)S(1)} copy-done((bf16[2,256,128]{2,1,0:T(8,128)(2,1)S(1)}, bf16[2,256,128]{2,1,0:T(8,128)(2,1)}, u32[]{:S(2)}) %copy-start.1) | copy-done | bytes 131096
  22.3 0.0 copy-start.2
  22.3 0.9 %copy-done.2 = bf16[4,128,128]{2,1,0:T(8,128)(2,1)S(1)} copy-done((bf16[4,128,128]{2,1,0:T(8,128)(2,1)S(1)}, bf16[4,128,128]{2,1,0:T(8,128)(2,1)}, u32[]{:S(2)}) %copy-start.2) | copy-done | bytes 131096
  23.2 0.0 copy-start.3
  23.2 0.7 %copy-done.3 = f32[4,128]{1,0:T(4,128)S(1)} copy-done((f32[4,128]{1,0:T(4,128)S(1)}, f32[4,128]{1,0:T(4,128)}, u32[]{:S(2)}) %copy-start.3) | copy-done | bytes 2072
  23.9 0.0 copy-start.4
  23.9 0.7 %copy-done.4 = s32[2]{0:T(128)S(1)} copy-done((s32[2]{0:T(128)S(1)}, s32[2]{0:T(128)}, u32[]{:S(2)}) %copy-start.4) | copy-done | bytes 32
  24.6 11.7 %shard_map.118 = (bf16[8,8,128]{2,1,0:T(8,128)(2,1)}, f32[2,256]{1,0:T(2,128)}, f32[2,256,128]{2,1,0:T(8,128)}, f32[4,128]{1,0:T(4,128)}, f32[4,9,128,128]{3,2,1,0:T(8,128)}, /*index=5*/f32[4,128,128]{2,1,0:T(8,128)}) custom-call(s32[2]{0:T(128)S(1)} %copy-done.4, bf16[320,128]{1,0:T(8,128)(2,1)S(1)} %concatenate.8.refs_0_, ...), custom_call_target="tpu_custom_call" | custom-call | tf_op jit(solution)/shard_map/pallas_call | solution.py:467
  (1 shorter events, 0.0 us)
Async XLA Ops:
  2.0 6.5 %collective-permute-start.2 = (bf16[80,128]{1,0:T(8,128)(2,1)S(1)}, bf16[80,128]{1,0:T(8,128)(2,1)S(1)}, u32[]{:S(2)}, u32[]{:S(2)}) collective-permute-start(bf16[80,128]{1,0:T(8,128)(2,1)S(1)} %pad_maximum_fusion), channel_id=1, source_target_pairs={{0,12},{4,0},{8,4},{12,8},{1,13},{5,1},{9,5},{13,9},{2,14},{6,2},{... | collective-permute-start | bytes 61448 | tf_op jit(solution)/shard_map/ppermute | solution.py:456
  7.1 4.7 %collective-permute-start.1 = (bf16[80,128]{1,0:T(8,128)(2,1)S(1)}, bf16[80,128]{1,0:T(8,128)(2,1)S(1)}, u32[]{:S(2)}, u32[]{:S(2)}) collective-permute-start(bf16[80,128]{1,0:T(8,128)(2,1)S(1)} %pad_maximum_fusion), channel_id=1, source_target_pairs={{0,8},{4,12},{8,0},{12,4},{1,9},{5,13},{9,1},{13,5},{2,10},{6,14},... | collective-permute-start | bytes 61448 | tf_op jit(solution)/shard_map/ppermute | solution.py:456
  7.1 5.6 %collective-permute-start = (bf16[80,128]{1,0:T(8,128)(2,1)S(1)}, bf16[80,128]{1,0:T(8,128)(2,1)S(1)}, u32[]{:S(2)}, u32[]{:S(2)}) collective-permute-start(bf16[80,128]{1,0:T(8,128)(2,1)S(1)} %pad_maximum_fusion), channel_id=1, source_target_pairs={{0,4},{4,8},{8,12},{12,0},{1,5},{5,9},{9,13},{13,1},{2,6},{6,10},{... | collective-permute-start | bytes 61448 | tf_op jit(solution)/shard_map/ppermute | solution.py:456
  13.6 2.1 %collective-permute-start.5 = (bf16[320,128]{1,0:T(8,128)(2,1)S(1)}, bf16[320,128]{1,0:T(8,128)(2,1)S(1)}, u32[]{:S(2)}, u32[]{:S(2)}) collective-permute-start(bf16[320,128]{1,0:T(8,128)(2,1)S(1)} %concatenate.8.refs_0_), channel_id=1, source_target_pairs={{0,3},{1,0},{2,1},{3,2},{4,7},{5,4},{6,5},{7,6},{8,11},{9,8},{10,9... | collective-permute-start | bytes 245768 | tf_op jit(solution)/shard_map/ppermute | solution.py:456
  13.6 6.4 %collective-permute-start.4 = (bf16[320,128]{1,0:T(8,128)(2,1)S(1)}, bf16[320,128]{1,0:T(8,128)(2,1)S(1)}, u32[]{:S(2)}, u32[]{:S(2)}) collective-permute-start(bf16[320,128]{1,0:T(8,128)(2,1)S(1)} %concatenate.8.refs_0_), channel_id=1, source_target_pairs={{0,2},{1,3},{2,0},{3,1},{4,6},{5,7},{6,4},{7,5},{8,10},{9,11},{10,... | collective-permute-start | bytes 245768 | tf_op jit(solution)/shard_map/ppermute | solution.py:456
  15.2 5.0 %collective-permute-start.3 = (bf16[320,128]{1,0:T(8,128)(2,1)S(1)}, bf16[320,128]{1,0:T(8,128)(2,1)S(1)}, u32[]{:S(2)}, u32[]{:S(2)}) collective-permute-start(bf16[320,128]{1,0:T(8,128)(2,1)S(1)} %concatenate.8.refs_0_), channel_id=1, source_target_pairs={{0,1},{1,2},{2,3},{3,0},{4,5},{5,6},{6,7},{7,4},{8,9},{9,10},{10,1... | collective-permute-start | bytes 245768 | tf_op jit(solution)/shard_map/ppermute | solution.py:456
  20.1 1.3 %copy-start = (bf16[4,3,3,128,128]{4,3,2,1,0:T(8,128)(2,1)S(1)}, bf16[4,3,3,128,128]{4,3,2,1,0:T(8,128)(2,1)}, u32[]{:S(2)}) copy-start(bf16[4,3,3,128,128]{4,3,2,1,0:T(8,128)(2,1)} %param.11) | copy-start | bytes 3538948
  21.4 0.9 %copy-start.1 = (bf16[2,256,128]{2,1,0:T(8,128)(2,1)S(1)}, bf16[2,256,128]{2,1,0:T(8,128)(2,1)}, u32[]{:S(2)}) copy-start(bf16[2,256,128]{2,1,0:T(8,128)(2,1)} %refs_4_.1) | copy-start | bytes 393220
  22.3 0.9 %copy-start.2 = (bf16[4,128,128]{2,1,0:T(8,128)(2,1)S(1)}, bf16[4,128,128]{2,1,0:T(8,128)(2,1)}, u32[]{:S(2)}) copy-start(bf16[4,128,128]{2,1,0:T(8,128)(2,1)} %refs_7_.1) | copy-start | bytes 393220
  23.2 0.7 %copy-start.3 = (f32[4,128]{1,0:T(4,128)S(1)}, f32[4,128]{1,0:T(4,128)}, u32[]{:S(2)}) copy-start(f32[4,128]{1,0:T(4,128)} %refs_5_.1) | copy-start | bytes 6148
  23.9 0.7 %copy-start.4 = (s32[2]{0:T(128)S(1)}, s32[2]{0:T(128)}, u32[]{:S(2)}) copy-start(s32[2]{0:T(128)} %lengths_ref.1) | copy-start | bytes 28

commit v2 on v0

--- a/solution.py
+++ b/solution.py
@@ -1,8 +1,11 @@
+import functools
 import math
 
 import jax
 import jax.numpy as jnp
 from jax import lax
+from jax.experimental import pallas as pl
+from jax.experimental.pallas import tpu as pltpu
 from jax.sharding import PartitionSpec as P
 
 LAYERS = 4
@@ -95,7 +98,7 @@
     return jnp.stack(terms)
 
 
-def body(seq_feat, lengths, embed_weight, norm_gain, conv_weight, proj_weight, pair_cotangent):
+def tiled_body(seq_feat, lengths, embed_weight, norm_gain, conv_weight, proj_weight, pair_cotangent):
     tile_rows = pair_cotangent.shape[0]
     tile_cols = pair_cotangent.shape[1]
     channels = pair_cotangent.shape[2]
@@ -211,6 +214,384 @@
     return (pair_output, seq_grad, embed_grad, gain_grad, conv_grad, proj_grad)
 
 
+NT = (((1,), (1,)), ((), ()))
+TN = (((0,), (0,)), ((), ()))
+NN = (((1,), (0,)), ((), ()))
+
+
+def dot(a, b, dims):
+    return lax.dot_general(a, b, dims, preferred_element_type=jnp.float32)
+
+
+def most_live(residues):
+    return residues - residues // 4
+
+
+CHUNK = 8
+
+
+def mix_parts(height):
+    return [slice(0, height)]
+
+
+def in_hbm(x):
+    return pltpu.with_memory_space_constraint(x, pltpu.HBM)
+
+
+def pack_kernel(seq_ref, tile_ref, out_ref):
+    rows, channels = out_ref.shape
+    tile = tile_ref.shape[0] * tile_ref.shape[1]
+    out_ref[:tile, :] = tile_ref[...].reshape(tile, channels)
+    seq = seq_ref[...].astype(jnp.float32)
+    own, features = seq.shape
+    parts = [seq[:, k : k + channels] for k in range(0, features, channels)]
+    parts.append(jnp.zeros((rows - tile - own * len(parts), channels), jnp.float32))
+    out_ref[tile:, :] = jnp.concatenate(parts, axis=0).astype(out_ref.dtype)
+
+
+def setup_kernel(*refs):
+    lengths_hbm, refs = refs[0], refs[1:]
+    half = (len(refs) - 3) // 2
+    live_ref, lengths, sem = refs[half], refs[-2], refs[-1]
+    copies = [
+        pltpu.make_async_copy(refs[k], refs[half + 1 + k], sem.at[k]) for k in range(half)
+    ]
+    count_copy = pltpu.make_async_copy(lengths_hbm, lengths, sem.at[half])
+    for copy in [count_copy] + copies:
+        copy.start()
+    pixel = jnp.maximum(
+        lax.broadcasted_iota(jnp.int32, live_ref.shape, 0),
+        lax.broadcasted_iota(jnp.int32, live_ref.shape, 1),
+    )
+    count_copy.wait()
+    live_ref[...] = (pixel < lengths[0]).astype(live_ref.dtype)
+    for copy in copies:
+        copy.wait()
+
+
+def block_kernel(grid_rows, grid_cols, *refs):
+    pieces, refs = refs[:2], refs[2:]
+    live, embed, gains, weights, proj = refs[:5]
+    (pair_hbm, seq_grad_hbm, embed_grad_hbm, gain_grad_hbm, conv_grad_hbm, proj_grad_hbm) = refs[5:11]
+    (
+        stream,
+        back,
+        shifted,
+        taps,
+        mixed,
+        normed,
+        inv,
+        slope,
+        squashed,
+        conv_slope,
+        excited,
+        masked,
+        spread,
+        seq_lo,
+        seq_hi,
+        pair_ref,
+        seq_grad_ref,
+        embed_grad_ref,
+        gain_grad_ref,
+        conv_grad,
+        proj_grad_ref,
+        sem,
+        grad_sem,
+    ) = refs[11:]
+    tile_rows, tile_cols, channels = pair_ref.shape
+    residues = tile_rows * grid_rows
+    own = seq_grad_ref.shape[0]
+    height = most_live(residues)
+    count = height * height
+    margin = 2 ** (LAYERS - 1)
+    pad = margin * height
+    chunks = [slice(k * CHUNK, (k + 1) * CHUNK) for k in range(height // CHUNK)]
+    row, col = lax.axis_index("row"), lax.axis_index("col")
+    stores = []
+
+    def store(source, target, semaphore):
+        copy = pltpu.make_async_copy(source, target, semaphore)
+        copy.start()
+        stores.append(copy)
+
+    stream[...] = jnp.zeros_like(stream)
+    shifted[...] = jnp.zeros_like(shifted)
+    for ref in (taps, mixed):
+        ref[:pad, :] = jnp.zeros((pad, ref.shape[1]), ref.dtype)
+        ref[pad + count :, :] = jnp.zeros((pad, ref.shape[1]), ref.dtype)
+
+    piece_rows = pieces[0].shape[0] // (2 * grid_rows)
+    tile = tile_rows * tile_cols
+    for step_col in range(grid_cols):
+        source_col = lax.bitwise_xor(col, step_col)
+        for step_row in range(grid_rows):
+            source_row = lax.rem(row + grid_rows - step_row, grid_rows)
+            first = (step_col // 2 * grid_rows + step_row) * piece_rows
+            piece = pieces[step_col % 2][first : first + piece_rows, :].astype(jnp.float32)
+            back[
+                pl.ds(pl.multiple_of(source_row * tile_rows, tile_rows), tile_rows),
+                pl.ds(pl.multiple_of(source_col * tile_cols, tile_cols), tile_cols),
+                :,
+            ] = piece[:tile].reshape(tile_rows, tile_cols, channels)
+            owner = source_row * grid_cols + source_col
+            spread[pl.ds(pl.multiple_of(owner * 8, 8), 8), :] = piece[tile : tile + 8]
+    owners = grid_rows * grid_cols
+    for k in range(own):
+        seq_lo[pl.ds(k, owners, stride=own), :] = spread[pl.ds(k, owners, stride=8), :]
+        seq_hi[pl.ds(k, owners, stride=own), :] = spread[pl.ds(own + k, owners, stride=8), :]
+    seq = jnp.concatenate([seq_lo[...], seq_hi[...]], axis=1).astype(jnp.bfloat16)
+
+    def get(ref, part):
+        return ref[part, :height, :].reshape(-1, channels)
+
+    def put(ref, part, value):
+        ref[part, :height, :] = value.reshape(CHUNK, height, channels)
+
+    row_emb = dot(seq, embed[0], NN).astype(jnp.bfloat16).astype(jnp.float32)
+    col_emb = dot(seq, embed[1], NN).astype(jnp.bfloat16).astype(jnp.float32)
+    for part in chunks:
+        stream[part, :height, :] = live[part, :height, :] * (
+            row_emb[part, None, :] + col_emb[None, :height, :]
+        )
+
+    def lane_mean(x):
+        return jnp.mean(x, axis=-1, keepdims=True)
+
+    def flat(part):
+        return slice(part.start * height, part.stop * height)
+
+    def moved(rows, by):
+        return slice(pad + rows.start + by * height, pad + rows.stop + by * height)
+
+    def store_shifted(part, value):
+        shifted[part, margin : margin + height, :] = value.reshape(CHUNK, height, channels)
+
+    def fill_taps(part, spacing):
+        for b in (-1, 0, 1):
+            start = margin + b * spacing
+            value = shifted[part, start : start + height, :].reshape(-1, channels)
+            taps[moved(flat(part), 0), (b + 1) * channels : (b + 2) * channels] = value.astype(
+                jnp.bfloat16
+            )
+
+    def mix(part, matrix, dims):
+        rows = moved(flat(part), 0)
+        mixed[rows, :] = dot(taps[rows, :], matrix, dims)
+
+    def gather_rows(part, spacing):
+        return sum(
+            mixed[moved(flat(part), a * spacing), (a + 1) * channels : (a + 2) * channels]
+            for a in (-1, 0, 1)
+        )
+
+    def block(layer, a, b):
+        first = (3 * a + b) * channels
+        return weights[layer, first : first + channels, :]
+
+    for layer in range(LAYERS):
+        spacing = 2**layer
+        gain = gains[layer : layer + 1, :]
+        for part in chunks:
+            value = get(stream, part)
+            centred = value - lane_mean(value)
+            inv_std = lax.rsqrt(lane_mean(centred * centred) + eps)
+            normalized = centred * inv_std
+            scaled = normalized * gain
+            decay = jnp.exp(jnp.minimum(scaled, 0.0))
+            activated = jnp.maximum(scaled, 0.0) + (decay - 1.0)
+            rows = flat(part)
+            normed[layer, rows, :] = normalized
+            inv[layer, rows, :] = jnp.broadcast_to(inv_std, normalized.shape)
+            slope[layer, rows, :] = decay * get(live, part)
+            store_shifted(part, activated)
+            squashed[layer, rows, :] = activated.astype(jnp.bfloat16)
+            fill_taps(part, spacing)
+        wide = jnp.concatenate(
+            [jnp.concatenate([block(layer, a, b) for b in range(3)], axis=0) for a in range(3)],
+            axis=1,
+        )
+        for part in mix_parts(height):
+            mix(part, wide, NN)
+        for part in chunks:
+            convolved = gather_rows(part, spacing)
+            decay = jnp.exp(jnp.minimum(convolved, 0.0))
+            rows = flat(part)
+            conv_slope[layer, rows, :] = decay
+            hidden = (jnp.maximum(convolved, 0.0) + (decay - 1.0)).astype(jnp.bfloat16)
+            excited[layer, rows, :] = hidden
+            update = dot(hidden, proj[layer], NN)
+            put(stream, part, get(stream, part) + get(live, part) * update)
+
+    pair_ref[...] = stream[
+        pl.ds(pl.multiple_of(row * tile_rows, tile_rows), tile_rows),
+        pl.ds(pl.multiple_of(col * tile_cols, tile_cols), tile_cols),
+        :,
+    ].astype(jnp.bfloat16)
+    store(pair_ref, pair_hbm, sem.at[0])
+
+    grad_scale = 1.0 / residues
+    for part in chunks:
+        put(back, part, get(back, part) * get(live, part))
+    for layer in reversed(range(LAYERS)):
+        spacing = 2**layer
+        gain = gains[layer : layer + 1, :]
+        for part in chunks:
+            grad = get(back, part).astype(jnp.bfloat16)
+            rows = flat(part)
+            masked[rows, :] = grad
+            store_shifted(part, dot(grad, proj[layer], NT) * conv_slope[layer, rows, :])
+            fill_taps(part, -spacing)
+        wide = jnp.concatenate(
+            [jnp.concatenate([block(layer, a, b) for b in range(3)], axis=1) for a in range(3)],
+            axis=0,
+        )
+        for part in mix_parts(height):
+            mix(part, wide, NT)
+        gain_total = jnp.zeros((1, channels), jnp.float32)
+        for part in chunks:
+            rows = flat(part)
+            normalized = normed[layer, rows, :]
+            d_scaled = gather_rows(part, -spacing) * slope[layer, rows, :]
+            gain_total = gain_total + jnp.sum(d_scaled * normalized, axis=0, keepdims=True)
+            d_norm = d_scaled * gain
+            delta = inv[layer, rows, :] * (
+                d_norm - lane_mean(d_norm) - normalized * lane_mean(d_norm * normalized)
+            )
+            put(back, part, get(back, part) + delta)
+        gain_grad_ref[layer : layer + 1, :] = gain_total * grad_scale
+        proj_grad_ref[layer] = dot(excited[layer], masked[...], TN) * grad_scale
+        every = slice(0, count)
+        for a in (-1, 0, 1):
+            part_grad = dot(squashed[layer], taps[moved(every, -a * spacing), :], TN) * grad_scale
+            for b in range(3):
+                conv_grad[layer, 3 * (a + 1) + b] = part_grad[:, b * channels : (b + 1) * channels]
+        store(conv_grad.at[layer], conv_grad_hbm.at[layer], grad_sem.at[0, layer])
+        store(proj_grad_ref.at[layer], proj_grad_hbm.at[layer], grad_sem.at[1, layer])
+
+    final = back[:height, :height, :]
+    rest = jnp.zeros((residues - height, channels), jnp.float32)
+    d_row = jnp.concatenate([jnp.sum(final, axis=1), rest], axis=0).astype(jnp.bfloat16)
+    d_col = jnp.concatenate([jnp.sum(final, axis=0), rest], axis=0).astype(jnp.bfloat16)
+    embed_grad_ref[0] = dot(seq, d_row, TN) * grad_scale
+    embed_grad_ref[1] = dot(seq, d_col, TN) * grad_scale
+    store(gain_grad_ref, gain_grad_hbm, sem.at[1])
+    store(embed_grad_ref, embed_grad_hbm, sem.at[2])
+    seq_grad = (dot(d_row, embed[0], NT) + dot(d_col, embed[1], NT)) / math.sqrt(residues)
+    first = own * (row * grid_cols + col)
+    for k in range(own):
+        chosen = lax.broadcasted_iota(jnp.int32, seq_grad.shape, 0) == first + k
+        seq_grad_ref[k : k + 1, :] = jnp.sum(
+            jnp.where(chosen, seq_grad, 0.0), axis=0, keepdims=True
+        )
+    store(seq_grad_ref, seq_grad_hbm, sem.at[3])
+    for copy in stores:
+        copy.wait()
+
+
+def replicated_body(
+    seq_feat, lengths, embed_weight, norm_gain, conv_weight, proj_weight, pair_cotangent
+):
+    tile_rows, tile_cols, channels = pair_cotangent.shape
+    grid_rows, grid_cols = lax.axis_size("row"), lax.axis_size("col")
+    residues = tile_rows * grid_rows
+    height = most_live(residues)
+    margin = 2 ** (LAYERS - 1)
+    own, features = seq_feat.shape
+    f32, bf16 = jnp.float32, jnp.bfloat16
+    vmem = pl.BlockSpec(memory_space=pltpu.VMEM)
+    hbm = pl.BlockSpec(memory_space=pltpu.HBM)
+    square = (residues, residues, channels)
+    payload = pl.pallas_call(
+        pack_kernel,
+        out_shape=pltpu.VMEM((tile_rows * tile_cols + 8, channels), bf16),
+    )(in_hbm(seq_feat), in_hbm(pair_cotangent))
+    payload = lax.optimization_barrier(payload)
+    held = (
+        embed_weight,
+        norm_gain,
+        conv_weight.reshape(LAYERS, 9 * channels, channels),
+        proj_weight,
+    )
+    live, *held = pl.pallas_call(
+        setup_kernel,
+        out_shape=[pltpu.VMEM(square, f32)] + [pltpu.VMEM(x.shape, x.dtype) for x in held],
+        in_specs=[hbm] * (1 + len(held)),
+        scratch_shapes=[
+            pltpu.SMEM(lengths.shape, jnp.int32),
+            pltpu.SemaphoreType.DMA((1 + len(held),)),
+        ],
+        cost_estimate=pl.CostEstimate(flops=0, bytes_accessed=4 * 2**20, transcendentals=0),
+    )(in_hbm(lengths), *[in_hbm(x) for x in held])
+
+    def swap(x, axis, count, bit):
+        return lax.ppermute(x, axis, [(i, i ^ bit) for i in range(count)])
+
+    def rotate(x, axis, count, step):
+        return lax.ppermute(x, axis, [(i, (i + step) % count) for i in range(count)])
+
+    columns = [payload] + [rotate(payload, "row", grid_rows, k) for k in range(1, grid_rows)]
+    columns, live, held = lax.optimization_barrier((columns, live, held))
+    column = lax.optimization_barrier(jnp.concatenate(columns, axis=0))
+    chip = jnp.concatenate([column, swap(column, "col", grid_cols, 2)], axis=0)
+    chip = lax.optimization_barrier(chip)
+    pieces = [chip, swap(chip, "col", grid_cols, 1)]
+    count = height * height
+    edge = margin * height
+    saved = (LAYERS, count, channels)
+    results = (
+        jax.ShapeDtypeStruct((tile_rows, tile_cols, channels), bf16),
+        jax.ShapeDtypeStruct((own, features), f32),
+        jax.ShapeDtypeStruct((2, features, channels), f32),
+        jax.ShapeDtypeStruct((LAYERS, channels), f32),
+        jax.ShapeDtypeStruct((LAYERS, 9, channels, channels), f32),
+        jax.ShapeDtypeStruct((LAYERS, channels, channels), f32),
+    )
+    outs = pl.pallas_call(
+        functools.partial(block_kernel, grid_rows, grid_cols),
+        out_shape=results,
+        in_specs=[vmem] * 7,
+        out_specs=(hbm,) * len(results),
+        scratch_shapes=[
+            pltpu.VMEM(square, f32),
+            pltpu.VMEM(square, f32),
+            pltpu.VMEM((height, height + 2 * margin, channels), f32),
+            pltpu.VMEM((count + 2 * edge, 3 * channels), bf16),
+            pltpu.VMEM((count + 2 * edge, 3 * channels), f32),
+            pltpu.VMEM(saved, f32),
+            pltpu.VMEM(saved, f32),
+            pltpu.VMEM(saved, f32),
+            pltpu.VMEM(saved, bf16),
+            pltpu.VMEM(saved, f32),
+            pltpu.VMEM(saved, bf16),
+            pltpu.VMEM((count, channels), bf16),
+            pltpu.VMEM((8 * grid_rows * grid_cols, channels), f32),
+            pltpu.VMEM((residues, channels), f32),
+            pltpu.VMEM((residues, channels), f32),
+            *[pltpu.VMEM(x.shape, x.dtype) for x in results],
+            pltpu.SemaphoreType.DMA((4,)),
+            pltpu.SemaphoreType.DMA((2, LAYERS)),
+        ],
+        compiler_params=pltpu.CompilerParams(vmem_limit_bytes=40 * 1024 * 1024),
+    )(*pieces, live, *held)
+    pair_output, seq_grad, embed_grad, gain_grad, conv_grad, proj_grad = outs
+    return (
+        pair_output,
+        seq_grad,
+        embed_grad,
+        gain_grad,
+        conv_grad.reshape(LAYERS, 3, 3, channels, channels),
+        proj_grad,
+    )
+
+
+def body(seq_feat, lengths, embed_weight, norm_gain, conv_weight, proj_weight, pair_cotangent):
+    residues = pair_cotangent.shape[0] * lax.axis_size("row")
+    plan = replicated_body if residues <= 32 else tiled_body
+    return plan(
+        seq_feat, lengths, embed_weight, norm_gain, conv_weight, proj_weight, pair_cotangent
+    )
+
+
 def solution(mesh):
     placed = (
         P(("groups", "row", "col"), None),

time: 351 us -> 25.9 us (0.07)
  waiting for transfers between devices: 127 us -> 7.34 us
  blocking collectives: 92.6 us -> 0 us
  starting transfers between devices: 73.6 us -> 7.62 us
  matrix products: 24.4 us -> 0 us
  between operations: 16.3 us -> 0.66 us
  Pallas kernels: 0 us -> 10 us
  local copies, waits for them, and re-layouts: 9.82 us -> 0 us
  other arithmetic: 6.18 us -> 0.02 us
    psum x1 -> x0, waiting for transfers between devices: 98.4 us -> none  [body(): lax.psum((gain_grad, conv_grad, proj_grad, embed_term), ('row', 'col'))]
    unnamed x2 -> x0, blocking collectives: 69.3 us -> none
    ppermute x32 -> x5, starting transfers between devices: 73.6 us -> 7.62 us  [the longest x3 6.06 us: rotate(): lax.ppermute(x, axis, [(i, (i + step) % count) for i in range(count)])]
    dot_general x126 -> x0, matrix products: 24.4 us -> none  [the longest x36 7.69 us: conv_weight_grad(): lax.dot_general(window.reshape(height * width, channels), flat_grad, (((0...]
    all_gather x1 -> x0, blocking collectives: 23.3 us -> none  [body(): gathered = lax.all_gather(seq_feat, ('row', 'col'), axis=0, tiled=True)]
    ppermute x32 -> x5, waiting for transfers between devices: 28.6 us -> 7.34 us  [the longest x2 4.22 us: swap(): return lax.ppermute(x, axis, [(i, i ^ bit) for i in range(count)])]
    pallas_call x0 -> x3, Pallas kernels: none -> 10 us  [the longest x1 7.85 us: replicated_body(): pl.pallas_call(functools.partial(block_kernel, grid_rows, grid_cols), out...]
    unnamed x20 -> x0, local copies, waits for them, and re-layouts: 7.07 us -> none
  transfers between devices with their start and end apart: 33 -> 5, of which waited for: 16 -> 4; matrix products, arithmetic and copies ran while one was open for 4% -> 0% of each run, Pallas kernels for 0% -> 6%
where the time goes in v2:
time: 25.9 us; the launch traced here: 25.6 us
  Pallas kernels  10 us (39%)
  starting transfers between devices  7.62 us (29%)
  waiting for transfers between devices  7.34 us (28%)
  between operations  0.66 us (3%)
    pallas_call x1, Pallas kernels, replicated_body(): pl.pallas_call(functools.partial(block_kernel, grid_rows, grid_cols), out...  7.85 us
    ppermute x3, starting transfers between devices, rotate(): lax.ppermute(x, axis, [(i, (i + step) % count) for i in range(count)])  6.06 us
    ppermute x2, waiting for transfers between devices, swap(): return lax.ppermute(x, axis, [(i, i ^ bit) for i in range(count)])  4.22 us
    ppermute x3, waiting for transfers between devices, rotate(): lax.ppermute(x, axis, [(i, (i + step) % count) for i in range(count)])  3.12 us
    ppermute x2, starting transfers between devices, swap(): return lax.ppermute(x, axis, [(i, i ^ bit) for i in range(count)])  1.56 us
    pallas_call x1, Pallas kernels, replicated_body(): pl.pallas_call(setup_kernel, out_shape=[pltpu.VMEM(square, f32)] + [pltpu...  1.41 us
    pallas_call x1, Pallas kernels, replicated_body(): pl.pallas_call(pack_kernel, out_shape=pltpu.VMEM((tile_rows * tile_cols +...  0.74 us
  transfers between devices with their start and end apart: 5, of which 4 were waited for; matrix products, arithmetic and copies ran while one was open for 0% of the time, Pallas kernels for 6%

profile of v2, /device:TPU:0, one launch (start us, length us, event | category | flops | bytes accessed | tf_op | source)
XLA Modules:
  0.0 25.6 jit_solution(7225959191985201761)
XLA Ops:
  0.6 0.7 %shard_map.118 = bf16[72,128]{1,0:T(8,128)(2,1)S(1)} custom-call(bf16[2,256]{1,0:T(2,128)(2,1)} %seq_ref.1, bf16[8,8,128]{2,1,0:T(8,128)(2,1)} %tile_ref.1), custom_call_target="tpu_custom_call" | custom-call | tf_op jit(solution)/shard_map/pallas_call | solution.py:504
  1.4 5.0 %collective-permute-start.2 = (bf16[72,128]{1,0:T(8,128)(2,1)S(1)}, bf16[72,128]{1,0:T(8,128)(2,1)S(1)}, u32[]{:S(2)}, u32[]{:S(2)}) collective-permute-start(bf16[72,128]{1,0:T(8,128)(2,1)S(1)} %shard_map.118), channel_id=1, source_target_pairs={{0,12},{4,0},{8,4},{12,8},{1,13},{5,1},{9,5},{13,9},{2,14},{6,2},{... | collective-permute-start | bytes 55304 | tf_op jit(solution)/shard_map/ppermute | solution.py:530
  6.4 0.0 collective-permute-start.1
  6.4 1.0 %collective-permute-start = (bf16[72,128]{1,0:T(8,128)(2,1)S(1)}, bf16[72,128]{1,0:T(8,128)(2,1)S(1)}, u32[]{:S(2)}, u32[]{:S(2)}) collective-permute-start(bf16[72,128]{1,0:T(8,128)(2,1)S(1)} %shard_map.118), channel_id=1, source_target_pairs={{0,4},{4,8},{8,12},{12,0},{1,5},{5,9},{9,13},{13,1},{2,6},{6,10},{... | collective-permute-start | bytes 55304 | tf_op jit(solution)/shard_map/ppermute | solution.py:530
  7.4 1.4 %shard_map.119 = (f32[32,32,128]{2,1,0:T(8,128)S(1)}, bf16[2,256,128]{2,1,0:T(8,128)(2,1)S(1)}, f32[4,128]{1,0:T(4,128)S(1)}, bf16[4,1152,128]{2,1,0:T(8,128)(2,1)S(1)}, bf16[4,128,128]{2,1,0:T(8,128)(2,1)S(1)}) custom-call(s32[2]{0:T(128)} %refs_0_.1, bf16[2,256,128]{2,1,0:T(8,128)(2,1)} %refs_1_.1, f32[4,128]{1,0:T(4,128)} %refs_2_.1, ...), custom_call_target="tpu_custom_call" | custom-call | bytes 4194304 | tf_op jit(solution)/shard_map/pallas_call | solution.py:515
  8.9 0.0 collective-permute-done.2
  8.9 2.2 %collective-permute-done.1 = bf16[72,128]{1,0:T(8,128)(2,1)S(1)} collective-permute-done((bf16[72,128]{1,0:T(8,128)(2,1)S(1)}, bf16[72,128]{1,0:T(8,128)(2,1)S(1)}, u32[]{:S(2)}, u32[]{:S(2)}) %collective-permute-start.1) | collective-permute-done | bytes 18464 | tf_op jit(solution)/shard_map/ppermute | solution.py:530
  11.1 0.9 %collective-permute-done = bf16[72,128]{1,0:T(8,128)(2,1)S(1)} collective-permute-done((bf16[72,128]{1,0:T(8,128)(2,1)S(1)}, bf16[72,128]{1,0:T(8,128)(2,1)S(1)}, u32[]{:S(2)}, u32[]{:S(2)}) %collective-permute-start) | collective-permute-done | bytes 18464 | tf_op jit(solution)/shard_map/ppermute | solution.py:530
  12.0 1.5 %collective-permute-start.3 = (bf16[288,128]{1,0:T(8,128)(2,1)S(1)}, bf16[288,128]{1,0:T(8,128)(2,1)S(1)}, u32[]{:S(2)}, u32[]{:S(2)}) collective-permute-start(bf16[288,128]{1,0:T(8,128)(2,1)S(1)} %pad_maximum_fusion.1), channel_id=1, source_target_pairs={{0,2},{1,3},{2,0},{3,1},{4,6},{5,7},{6,4},{7,5},{8,10},{9,11},{10,... | collective-permute-start | bytes 221192 | tf_op jit(solution)/shard_map/ppermute | solution.py:527
  13.5 2.9 %collective-permute-done.3 = bf16[288,128]{1,0:T(8,128)(2,1)S(1)} collective-permute-done((bf16[288,128]{1,0:T(8,128)(2,1)S(1)}, bf16[288,128]{1,0:T(8,128)(2,1)S(1)}, u32[]{:S(2)}, u32[]{:S(2)}) %collective-permute-start.3) | collective-permute-done | bytes 73760 | tf_op jit(solution)/shard_map/ppermute | solution.py:527
  16.4 0.1 collective-permute-start.4
  16.4 1.4 %collective-permute-done.4.refs_1_ = bf16[576,128]{1,0:T(8,128)(2,1)S(1)} collective-permute-done((bf16[576,128]{1,0:T(8,128)(2,1)S(1)}, bf16[576,128]{1,0:T(8,128)(2,1)S(1)}, u32[]{:S(2)}, u32[]{:S(2)}) %collective-permute-start.4) | collective-permute-done | bytes 147488 | tf_op jit(solution)/shard_map/ppermute | solution.py:527
  17.8 7.8 %shard_map.120 = (bf16[8,8,128]{2,1,0:T(8,128)(2,1)}, f32[2,256]{1,0:T(2,128)}, f32[2,256,128]{2,1,0:T(8,128)}, f32[4,128]{1,0:T(4,128)}, f32[4,9,128,128]{3,2,1,0:T(8,128)}, /*index=5*/f32[4,128,128]{2,1,0:T(8,128)}) custom-call(bf16[576,128]{1,0:T(8,128)(2,1)S(1)} %pad_maximum_fusion.refs_0_, bf16[576,128]{1,0:T(8,128)(2,1)S(1)} %collective-permute-done.4.refs_1_, ...), custom_call_target="tpu_custom_call" | custom-call | tf_op jit(solution)/shard_map/pallas_call | solution.py:549
  (2 shorter events, 0.0 us)
Async XLA Ops:
  1.4 7.5 %collective-permute-start.2 = (bf16[72,128]{1,0:T(8,128)(2,1)S(1)}, bf16[72,128]{1,0:T(8,128)(2,1)S(1)}, u32[]{:S(2)}, u32[]{:S(2)}) collective-permute-start(bf16[72,128]{1,0:T(8,128)(2,1)S(1)} %shard_map.118), channel_id=1, source_target_pairs={{0,12},{4,0},{8,4},{12,8},{1,13},{5,1},{9,5},{13,9},{2,14},{6,2},{... | collective-permute-start | bytes 55304 | tf_op jit(solution)/shard_map/ppermute | solution.py:530
  6.4 4.7 %collective-permute-start.1 = (bf16[72,128]{1,0:T(8,128)(2,1)S(1)}, bf16[72,128]{1,0:T(8,128)(2,1)S(1)}, u32[]{:S(2)}, u32[]{:S(2)}) collective-permute-start(bf16[72,128]{1,0:T(8,128)(2,1)S(1)} %shard_map.118), channel_id=1, source_target_pairs={{0,8},{4,12},{8,0},{12,4},{1,9},{5,13},{9,1},{13,5},{2,10},{6,14},... | collective-permute-start | bytes 55304 | tf_op jit(solution)/shard_map/ppermute | solution.py:530
  6.4 5.6 %collective-permute-start = (bf16[72,128]{1,0:T(8,128)(2,1)S(1)}, bf16[72,128]{1,0:T(8,128)(2,1)S(1)}, u32[]{:S(2)}, u32[]{:S(2)}) collective-permute-start(bf16[72,128]{1,0:T(8,128)(2,1)S(1)} %shard_map.118), channel_id=1, source_target_pairs={{0,4},{4,8},{8,12},{12,0},{1,5},{5,9},{9,13},{13,1},{2,6},{6,10},{... | collective-permute-start | bytes 55304 | tf_op jit(solution)/shard_map/ppermute | solution.py:530
  12.0 4.4 %collective-permute-start.3 = (bf16[288,128]{1,0:T(8,128)(2,1)S(1)}, bf16[288,128]{1,0:T(8,128)(2,1)S(1)}, u32[]{:S(2)}, u32[]{:S(2)}) collective-permute-start(bf16[288,128]{1,0:T(8,128)(2,1)S(1)} %pad_maximum_fusion.1), channel_id=1, source_target_pairs={{0,2},{1,3},{2,0},{3,1},{4,6},{5,7},{6,4},{7,5},{8,10},{9,11},{10,... | collective-permute-start | bytes 221192 | tf_op jit(solution)/shard_map/ppermute | solution.py:527
  16.4 1.4 %collective-permute-start.4 = (bf16[576,128]{1,0:T(8,128)(2,1)S(1)}, bf16[576,128]{1,0:T(8,128)(2,1)S(1)}, u32[]{:S(2)}, u32[]{:S(2)}) collective-permute-start(bf16[576,128]{1,0:T(8,128)(2,1)S(1)} %pad_maximum_fusion.refs_0_), channel_id=1, source_target_pairs={{0,1},{1,0},{2,3},{3,2},{4,5},{5,4},{6,7},{7,6},{8,9},{9,8},{10,11... | collective-permute-start | bytes 442376 | tf_op jit(solution)/shard_map/ppermute | solution.py:527

commit v3 on v2

--- a/solution.py
+++ b/solution.py
@@ -325,7 +325,7 @@
     for step_col in range(grid_cols):
         source_col = lax.bitwise_xor(col, step_col)
         for step_row in range(grid_rows):
-            source_row = lax.rem(row + grid_rows - step_row, grid_rows)
+            source_row = lax.rem(row + step_row, grid_rows)
             first = (step_col // 2 * grid_rows + step_row) * piece_rows
             piece = pieces[step_col % 2][first : first + piece_rows, :].astype(jnp.float32)
             back[
@@ -506,6 +506,15 @@
         out_shape=pltpu.VMEM((tile_rows * tile_cols + 8, channels), bf16),
     )(in_hbm(seq_feat), in_hbm(pair_cotangent))
     payload = lax.optimization_barrier(payload)
+    def swap(x, axis, count, bit):
+        return lax.ppermute(x, axis, [(i, i ^ bit) for i in range(count)])
+
+    def rotate(x, axis, count, step):
+        return lax.ppermute(x, axis, [(i, (i + step) % count) for i in range(count)])
+
+    turns = [rotate(payload, "row", grid_rows, k) for k in reversed(range(1, grid_rows))]
+    column = lax.optimization_barrier(jnp.concatenate([payload] + turns, axis=0))
+    column, lengths = lax.optimization_barrier((column, lengths))
     held = (
         embed_weight,
         norm_gain,
@@ -523,17 +532,9 @@
         cost_estimate=pl.CostEstimate(flops=0, bytes_accessed=4 * 2**20, transcendentals=0),
     )(in_hbm(lengths), *[in_hbm(x) for x in held])
 
-    def swap(x, axis, count, bit):
-        return lax.ppermute(x, axis, [(i, i ^ bit) for i in range(count)])
-
-    def rotate(x, axis, count, step):
-        return lax.ppermute(x, axis, [(i, (i + step) % count) for i in range(count)])
-
-    columns = [payload] + [rotate(payload, "row", grid_rows, k) for k in range(1, grid_rows)]
-    columns, live, held = lax.optimization_barrier((columns, live, held))
-    column = lax.optimization_barrier(jnp.concatenate(columns, axis=0))
-    chip = jnp.concatenate([column, swap(column, "col", grid_cols, 2)], axis=0)
-    chip = lax.optimization_barrier(chip)
+    chip = [column, swap(column, "col", grid_cols, 2)]
+    chip, live, held = lax.optimization_barrier((chip, live, held))
+    chip = lax.optimization_barrier(jnp.concatenate(chip, axis=0))
     pieces = [chip, swap(chip, "col", grid_cols, 1)]
     count = height * height
     edge = margin * height

time: 25.9 us -> 24.6 us (0.950)
  waiting for transfers between devices: 7.34 us -> 5.21 us
  starting transfers between devices: 7.62 us -> 8.52 us
    ppermute x2, waiting for transfers between devices: 4.22 us -> 2.8 us  [swap(): return lax.ppermute(x, axis, [(i, i ^ bit) for i in range(count)])]
    ppermute x3, starting transfers between devices: 6.06 us -> 6.96 us  [rotate(): lax.ppermute(x, axis, [(i, (i + step) % count) for i in range(count)])]
    ppermute x3, waiting for transfers between devices: 3.12 us -> 2.41 us  [rotate(): lax.ppermute(x, axis, [(i, (i + step) % count) for i in range(count)])]
where the time goes in v3:
time: 24.6 us; the launch traced here: 24.4 us
  Pallas kernels  9.99 us (41%)
  starting transfers between devices  8.52 us (35%)
  waiting for transfers between devices  5.21 us (21%)
  between operations  0.66 us (3%)
    pallas_call x1, Pallas kernels, replicated_body(): pl.pallas_call(functools.partial(block_kernel, grid_rows, grid_cols), out...  7.84 us
    ppermute x3, starting transfers between devices, rotate(): lax.ppermute(x, axis, [(i, (i + step) % count) for i in range(count)])  6.96 us
    ppermute x2, waiting for transfers between devices, swap(): return lax.ppermute(x, axis, [(i, i ^ bit) for i in range(count)])  2.8 us
    ppermute x3, waiting for transfers between devices, rotate(): lax.ppermute(x, axis, [(i, (i + step) % count) for i in range(count)])  2.41 us
    ppermute x2, starting transfers between devices, swap(): return lax.ppermute(x, axis, [(i, i ^ bit) for i in range(count)])  1.56 us
    pallas_call x1, Pallas kernels, replicated_body(): pl.pallas_call(setup_kernel, out_shape=[pltpu.VMEM(square, f32)] + [pltpu...  1.41 us
    pallas_call x1, Pallas kernels, replicated_body(): pl.pallas_call(pack_kernel, out_shape=pltpu.VMEM((tile_rows * tile_cols +...  0.74 us
  transfers between devices with their start and end apart: 5, of which 4 were waited for; matrix products, arithmetic and copies ran while one was open for 0% of the time, Pallas kernels for 6%

profile of v3, /device:TPU:0, one launch (start us, length us, event | category | flops | bytes accessed | tf_op | source)
XLA Modules:
  0.0 24.4 jit_solution(13071105980135505960)
XLA Ops:
  0.6 0.7 %shard_map.118 = bf16[72,128]{1,0:T(8,128)(2,1)S(1)} custom-call(bf16[2,256]{1,0:T(2,128)(2,1)} %seq_ref.1, bf16[8,8,128]{2,1,0:T(8,128)(2,1)} %tile_ref.1), custom_call_target="tpu_custom_call" | custom-call | tf_op jit(solution)/shard_map/pallas_call | solution.py:504
  1.4 3.0 %collective-permute-start.2 = (bf16[72,128]{1,0:T(8,128)(2,1)S(1)}, bf16[72,128]{1,0:T(8,128)(2,1)S(1)}, u32[]{:S(2)}, u32[]{:S(2)}) collective-permute-start(bf16[72,128]{1,0:T(8,128)(2,1)S(1)} %shard_map.118), channel_id=1, source_target_pairs={{0,4},{4,8},{8,12},{12,0},{1,5},{5,9},{9,13},{13,1},{2,6},{6,10},{... | collective-permute-start | bytes 55304 | tf_op jit(solution)/shard_map/ppermute | solution.py:513
  4.4 2.6 %collective-permute-start.1 = (bf16[72,128]{1,0:T(8,128)(2,1)S(1)}, bf16[72,128]{1,0:T(8,128)(2,1)S(1)}, u32[]{:S(2)}, u32[]{:S(2)}) collective-permute-start(bf16[72,128]{1,0:T(8,128)(2,1)S(1)} %shard_map.118), channel_id=1, source_target_pairs={{0,8},{4,12},{8,0},{12,4},{1,9},{5,13},{9,1},{13,5},{2,10},{6,14},... | collective-permute-start | bytes 55304 | tf_op jit(solution)/shard_map/ppermute | solution.py:513
  7.0 1.3 %collective-permute-start = (bf16[72,128]{1,0:T(8,128)(2,1)S(1)}, bf16[72,128]{1,0:T(8,128)(2,1)S(1)}, u32[]{:S(2)}, u32[]{:S(2)}) collective-permute-start(bf16[72,128]{1,0:T(8,128)(2,1)S(1)} %shard_map.118), channel_id=1, source_target_pairs={{0,12},{4,0},{8,4},{12,8},{1,13},{5,1},{9,5},{13,9},{2,14},{6,2},{... | collective-permute-start | bytes 55304 | tf_op jit(solution)/shard_map/ppermute | solution.py:513
  8.3 0.0 collective-permute-done.2
  8.3 0.8 %collective-permute-done.1 = bf16[72,128]{1,0:T(8,128)(2,1)S(1)} collective-permute-done((bf16[72,128]{1,0:T(8,128)(2,1)S(1)}, bf16[72,128]{1,0:T(8,128)(2,1)S(1)}, u32[]{:S(2)}, u32[]{:S(2)}) %collective-permute-start.1) | collective-permute-done | bytes 18464 | tf_op jit(solution)/shard_map/ppermute | solution.py:513
  9.2 1.6 %collective-permute-done = bf16[72,128]{1,0:T(8,128)(2,1)S(1)} collective-permute-done((bf16[72,128]{1,0:T(8,128)(2,1)S(1)}, bf16[72,128]{1,0:T(8,128)(2,1)S(1)}, u32[]{:S(2)}, u32[]{:S(2)}) %collective-permute-start) | collective-permute-done | bytes 18464 | tf_op jit(solution)/shard_map/ppermute | solution.py:513
  10.8 1.5 %collective-permute-start.3 = (bf16[288,128]{1,0:T(8,128)(2,1)S(1)}, bf16[288,128]{1,0:T(8,128)(2,1)S(1)}, u32[]{:S(2)}, u32[]{:S(2)}) collective-permute-start(bf16[288,128]{1,0:T(8,128)(2,1)S(1)} %pad_maximum_fusion.1), channel_id=1, source_target_pairs={{0,2},{1,3},{2,0},{3,1},{4,6},{5,7},{6,4},{7,5},{8,10},{9,11},{10,... | collective-permute-start | bytes 221192 | tf_op jit(solution)/shard_map/ppermute | solution.py:510
  12.2 1.4 %shard_map.119 = (f32[32,32,128]{2,1,0:T(8,128)S(1)}, bf16[2,256,128]{2,1,0:T(8,128)(2,1)S(1)}, f32[4,128]{1,0:T(4,128)S(1)}, bf16[4,1152,128]{2,1,0:T(8,128)(2,1)S(1)}, bf16[4,128,128]{2,1,0:T(8,128)(2,1)S(1)}) custom-call(s32[2]{0:T(128)} %refs_0_, bf16[2,256,128]{2,1,0:T(8,128)(2,1)} %refs_1_.1, f32[4,128]{1,0:T(4,128)} %refs_2_.1, ...), custom_call_target="tpu_custom_call" | custom-call | bytes 4194304 | tf_op jit(solution)/shard_map/pallas_call | solution.py:524
  13.7 1.4 %collective-permute-done.3 = bf16[288,128]{1,0:T(8,128)(2,1)S(1)} collective-permute-done((bf16[288,128]{1,0:T(8,128)(2,1)S(1)}, bf16[288,128]{1,0:T(8,128)(2,1)S(1)}, u32[]{:S(2)}, u32[]{:S(2)}) %collective-permute-start.3) | collective-permute-done | bytes 73760 | tf_op jit(solution)/shard_map/ppermute | solution.py:510
  15.1 0.1 collective-permute-start.4
  15.2 1.4 %collective-permute-done.4.refs_1_ = bf16[576,128]{1,0:T(8,128)(2,1)S(1)} collective-permute-done((bf16[576,128]{1,0:T(8,128)(2,1)S(1)}, bf16[576,128]{1,0:T(8,128)(2,1)S(1)}, u32[]{:S(2)}, u32[]{:S(2)}) %collective-permute-start.4) | collective-permute-done | bytes 147488 | tf_op jit(solution)/shard_map/ppermute | solution.py:510
  16.6 7.8 %shard_map.120 = (bf16[8,8,128]{2,1,0:T(8,128)(2,1)}, f32[2,256]{1,0:T(2,128)}, f32[2,256,128]{2,1,0:T(8,128)}, f32[4,128]{1,0:T(4,128)}, f32[4,9,128,128]{3,2,1,0:T(8,128)}, /*index=5*/f32[4,128,128]{2,1,0:T(8,128)}) custom-call(bf16[576,128]{1,0:T(8,128)(2,1)S(1)} %pad_maximum_fusion.refs_0_, bf16[576,128]{1,0:T(8,128)(2,1)S(1)} %collective-permute-done.4.refs_1_, ...), custom_call_target="tpu_custom_call" | custom-call | tf_op jit(solution)/shard_map/pallas_call | solution.py:550
  (2 shorter events, 0.0 us)
Async XLA Ops:
  1.4 7.0 %collective-permute-start.2 = (bf16[72,128]{1,0:T(8,128)(2,1)S(1)}, bf16[72,128]{1,0:T(8,128)(2,1)S(1)}, u32[]{:S(2)}, u32[]{:S(2)}) collective-permute-start(bf16[72,128]{1,0:T(8,128)(2,1)S(1)} %shard_map.118), channel_id=1, source_target_pairs={{0,4},{4,8},{8,12},{12,0},{1,5},{5,9},{9,13},{13,1},{2,6},{6,10},{... | collective-permute-start | bytes 55304 | tf_op jit(solution)/shard_map/ppermute | solution.py:513
  4.4 4.8 %collective-permute-start.1 = (bf16[72,128]{1,0:T(8,128)(2,1)S(1)}, bf16[72,128]{1,0:T(8,128)(2,1)S(1)}, u32[]{:S(2)}, u32[]{:S(2)}) collective-permute-start(bf16[72,128]{1,0:T(8,128)(2,1)S(1)} %shard_map.118), channel_id=1, source_target_pairs={{0,8},{4,12},{8,0},{12,4},{1,9},{5,13},{9,1},{13,5},{2,10},{6,14},... | collective-permute-start | bytes 55304 | tf_op jit(solution)/shard_map/ppermute | solution.py:513
  7.0 3.8 %collective-permute-start = (bf16[72,128]{1,0:T(8,128)(2,1)S(1)}, bf16[72,128]{1,0:T(8,128)(2,1)S(1)}, u32[]{:S(2)}, u32[]{:S(2)}) collective-permute-start(bf16[72,128]{1,0:T(8,128)(2,1)S(1)} %shard_map.118), channel_id=1, source_target_pairs={{0,12},{4,0},{8,4},{12,8},{1,13},{5,1},{9,5},{13,9},{2,14},{6,2},{... | collective-permute-start | bytes 55304 | tf_op jit(solution)/shard_map/ppermute | solution.py:513
  10.8 4.4 %collective-permute-start.3 = (bf16[288,128]{1,0:T(8,128)(2,1)S(1)}, bf16[288,128]{1,0:T(8,128)(2,1)S(1)}, u32[]{:S(2)}, u32[]{:S(2)}) collective-permute-start(bf16[288,128]{1,0:T(8,128)(2,1)S(1)} %pad_maximum_fusion.1), channel_id=1, source_target_pairs={{0,2},{1,3},{2,0},{3,1},{4,6},{5,7},{6,4},{7,5},{8,10},{9,11},{10,... | collective-permute-start | bytes 221192 | tf_op jit(solution)/shard_map/ppermute | solution.py:510
  15.1 1.4 %collective-permute-start.4 = (bf16[576,128]{1,0:T(8,128)(2,1)S(1)}, bf16[576,128]{1,0:T(8,128)(2,1)S(1)}, u32[]{:S(2)}, u32[]{:S(2)}) collective-permute-start(bf16[576,128]{1,0:T(8,128)(2,1)S(1)} %pad_maximum_fusion.refs_0_), channel_id=1, source_target_pairs={{0,1},{1,0},{2,3},{3,2},{4,5},{5,4},{6,7},{7,6},{8,9},{9,8},{10,11... | collective-permute-start | bytes 442376 | tf_op jit(solution)/shard_map/ppermute | solution.py:510

commit v4 on v3

--- a/solution.py
+++ b/solution.py
@@ -251,8 +251,8 @@
 
 def setup_kernel(*refs):
     lengths_hbm, refs = refs[0], refs[1:]
-    half = (len(refs) - 3) // 2
-    live_ref, lengths, sem = refs[half], refs[-2], refs[-1]
+    half = (len(refs) - 4) // 2
+    live_ref, mean_ref, lengths, sem = refs[half], refs[-3], refs[-2], refs[-1]
     copies = [
         pltpu.make_async_copy(refs[k], refs[half + 1 + k], sem.at[k]) for k in range(half)
     ]
@@ -267,14 +267,18 @@
     live_ref[...] = (pixel < lengths[0]).astype(live_ref.dtype)
     for copy in copies:
         copy.wait()
+    proj = refs[2 * half][...].astype(jnp.float32)
+    mean = jnp.mean(proj, axis=-1, keepdims=True)
+    mean_ref[...] = jnp.broadcast_to(mean, proj.shape).astype(mean_ref.dtype)
 
 
 def block_kernel(grid_rows, grid_cols, *refs):
     pieces, refs = refs[:2], refs[2:]
-    live, embed, gains, weights, proj = refs[:5]
-    (pair_hbm, seq_grad_hbm, embed_grad_hbm, gain_grad_hbm, conv_grad_hbm, proj_grad_hbm) = refs[5:11]
+    live, embed, gains, weights, proj, proj_mean = refs[:6]
+    (pair_hbm, seq_grad_hbm, embed_grad_hbm, gain_grad_hbm, conv_grad_hbm, proj_grad_hbm) = refs[6:12]
     (
         stream,
+        guess,
         back,
         shifted,
         taps,
@@ -297,7 +301,7 @@
         proj_grad_ref,
         sem,
         grad_sem,
-    ) = refs[11:]
+    ) = refs[12:]
     tile_rows, tile_cols, channels = pair_ref.shape
     residues = tile_rows * grid_rows
     own = seq_grad_ref.shape[0]
@@ -360,6 +364,12 @@
     def flat(part):
         return slice(part.start * height, part.stop * height)
 
+    row_mean = jnp.broadcast_to(lane_mean(row_emb), row_emb.shape)
+    col_mean = jnp.broadcast_to(lane_mean(col_emb), col_emb.shape)
+    for part in chunks:
+        first = live[part, :height, :] * (row_mean[part, None, :] + col_mean[None, :height, :])
+        guess[flat(part), :] = first.reshape(-1, channels)
+
     def moved(rows, by):
         return slice(pad + rows.start + by * height, pad + rows.stop + by * height)
 
@@ -376,7 +386,11 @@
 
     def mix(part, matrix, dims):
         rows = moved(flat(part), 0)
-        mixed[rows, :] = dot(taps[rows, :], matrix, dims)
+        edge = 2 * channels
+        low, high = (matrix[:edge], matrix[edge:])
+        if dims is NT:
+            low, high = (matrix[:, :edge], matrix[:, edge:])
+        mixed[rows, :] = dot(taps[rows, :edge], low, dims) + dot(taps[rows, edge:], high, dims)
 
     def gather_rows(part, spacing):
         return sum(
@@ -392,10 +406,11 @@
         spacing = 2**layer
         gain = gains[layer : layer + 1, :]
         for part in chunks:
-            value = get(stream, part)
-            centred = value - lane_mean(value)
-            inv_std = lax.rsqrt(lane_mean(centred * centred) + eps)
-            normalized = centred * inv_std
+            near = get(stream, part) - guess[flat(part), :]
+            offset = lane_mean(near)
+            variance = jnp.maximum(lane_mean(near * near) - offset * offset, 0.0)
+            inv_std = lax.rsqrt(variance + eps)
+            normalized = (near - offset) * inv_std
             scaled = normalized * gain
             decay = jnp.exp(jnp.minimum(scaled, 0.0))
             activated = jnp.maximum(scaled, 0.0) + (decay - 1.0)
@@ -419,8 +434,11 @@
             conv_slope[layer, rows, :] = decay
             hidden = (jnp.maximum(convolved, 0.0) + (decay - 1.0)).astype(jnp.bfloat16)
             excited[layer, rows, :] = hidden
-            update = dot(hidden, proj[layer], NN)
-            put(stream, part, get(stream, part) + get(live, part) * update)
+            both = jnp.concatenate([proj[layer], proj_mean[layer]], axis=1)
+            update = dot(hidden, both, NN)
+            alive = get(live, part)
+            put(stream, part, get(stream, part) + alive * update[:, :channels])
+            guess[rows, :] = guess[rows, :] + alive * update[:, channels:]
 
     pair_ref[...] = stream[
         pl.ds(pl.multiple_of(row * tile_rows, tile_rows), tile_rows),
@@ -523,7 +541,8 @@
     )
     live, *held = pl.pallas_call(
         setup_kernel,
-        out_shape=[pltpu.VMEM(square, f32)] + [pltpu.VMEM(x.shape, x.dtype) for x in held],
+        out_shape=[pltpu.VMEM(square, f32)]
+        + [pltpu.VMEM(x.shape, x.dtype) for x in held + (proj_weight,)],
         in_specs=[hbm] * (1 + len(held)),
         scratch_shapes=[
             pltpu.SMEM(lengths.shape, jnp.int32),
@@ -550,10 +569,11 @@
     outs = pl.pallas_call(
         functools.partial(block_kernel, grid_rows, grid_cols),
         out_shape=results,
-        in_specs=[vmem] * 7,
+        in_specs=[vmem] * 8,
         out_specs=(hbm,) * len(results),
         scratch_shapes=[
             pltpu.VMEM(square, f32),
+            pltpu.VMEM((count, channels), f32),
             pltpu.VMEM(square, f32),
             pltpu.VMEM((height, height + 2 * margin, channels), f32),
             pltpu.VMEM((count + 2 * edge, 3 * channels), bf16),

time: 24.6 us -> 24.1 us (0.980)
  Pallas kernels: 9.99 us -> 9.6 us
    pallas_call x1, Pallas kernels: 7.84 us -> 7.3 us  [replicated_body(): pl.pallas_call(functools.partial(block_kernel, grid_rows, grid_cols), out...]
  transfers between devices with their start and end apart: 5 -> 5, of which waited for: 4 -> 4; matrix products, arithmetic and copies ran while one was open for 0% -> 0% of each run, Pallas kernels for 6% -> 7%
where the time goes in v4:
time: 24.1 us; the launch traced here: 23.9 us
  Pallas kernels  9.6 us (40%)
  starting transfers between devices  8.52 us (35%)
  waiting for transfers between devices  5.07 us (21%)
  between operations  0.66 us (3%)
    pallas_call x1, Pallas kernels, replicated_body(): pl.pallas_call(functools.partial(block_kernel, grid_rows, grid_cols), out...  7.3 us
    ppermute x3, starting transfers between devices, rotate(): lax.ppermute(x, axis, [(i, (i + step) % count) for i in range(count)])  6.96 us
    ppermute x2, waiting for transfers between devices, swap(): return lax.ppermute(x, axis, [(i, i ^ bit) for i in range(count)])  2.66 us
    ppermute x3, waiting for transfers between devices, rotate(): lax.ppermute(x, axis, [(i, (i + step) % count) for i in range(count)])  2.41 us
    ppermute x2, starting transfers between devices, swap(): return lax.ppermute(x, axis, [(i, i ^ bit) for i in range(count)])  1.56 us
    pallas_call x1, Pallas kernels, replicated_body(): pl.pallas_call(setup_kernel, out_shape=[pltpu.VMEM(square, f32)] + [pltpu...  1.56 us
    pallas_call x1, Pallas kernels, replicated_body(): pl.pallas_call(pack_kernel, out_shape=pltpu.VMEM((tile_rows * tile_cols +...  0.74 us
  transfers between devices with their start and end apart: 5, of which 4 were waited for; matrix products, arithmetic and copies ran while one was open for 0% of the time, Pallas kernels for 7%

profile of v4, /device:TPU:0, one launch (start us, length us, event | category | flops | bytes accessed | tf_op | source)
XLA Modules:
  0.0 23.9 jit_solution(12024380001934133900)
XLA Ops:
  0.6 0.7 %shard_map.118 = bf16[72,128]{1,0:T(8,128)(2,1)S(1)} custom-call(bf16[2,256]{1,0:T(2,128)(2,1)} %seq_ref.1, bf16[8,8,128]{2,1,0:T(8,128)(2,1)} %tile_ref.1), custom_call_target="tpu_custom_call" | custom-call | tf_op jit(solution)/shard_map/pallas_call | solution.py:522
  1.4 3.0 %collective-permute-start.2 = (bf16[72,128]{1,0:T(8,128)(2,1)S(1)}, bf16[72,128]{1,0:T(8,128)(2,1)S(1)}, u32[]{:S(2)}, u32[]{:S(2)}) collective-permute-start(bf16[72,128]{1,0:T(8,128)(2,1)S(1)} %shard_map.118), channel_id=1, source_target_pairs={{0,4},{4,8},{8,12},{12,0},{1,5},{5,9},{9,13},{13,1},{2,6},{6,10},{... | collective-permute-start | bytes 55304 | tf_op jit(solution)/shard_map/ppermute | solution.py:531
  4.4 2.6 %collective-permute-start.1 = (bf16[72,128]{1,0:T(8,128)(2,1)S(1)}, bf16[72,128]{1,0:T(8,128)(2,1)S(1)}, u32[]{:S(2)}, u32[]{:S(2)}) collective-permute-start(bf16[72,128]{1,0:T(8,128)(2,1)S(1)} %shard_map.118), channel_id=1, source_target_pairs={{0,8},{4,12},{8,0},{12,4},{1,9},{5,13},{9,1},{13,5},{2,10},{6,14},... | collective-permute-start | bytes 55304 | tf_op jit(solution)/shard_map/ppermute | solution.py:531
  7.0 1.3 %collective-permute-start = (bf16[72,128]{1,0:T(8,128)(2,1)S(1)}, bf16[72,128]{1,0:T(8,128)(2,1)S(1)}, u32[]{:S(2)}, u32[]{:S(2)}) collective-permute-start(bf16[72,128]{1,0:T(8,128)(2,1)S(1)} %shard_map.118), channel_id=1, source_target_pairs={{0,12},{4,0},{8,4},{12,8},{1,13},{5,1},{9,5},{13,9},{2,14},{6,2},{... | collective-permute-start | bytes 55304 | tf_op jit(solution)/shard_map/ppermute | solution.py:531
  8.3 0.0 collective-permute-done.2
  8.3 0.8 %collective-permute-done.1 = bf16[72,128]{1,0:T(8,128)(2,1)S(1)} collective-permute-done((bf16[72,128]{1,0:T(8,128)(2,1)S(1)}, bf16[72,128]{1,0:T(8,128)(2,1)S(1)}, u32[]{:S(2)}, u32[]{:S(2)}) %collective-permute-start.1) | collective-permute-done | bytes 18464 | tf_op jit(solution)/shard_map/ppermute | solution.py:531
  9.2 1.6 %collective-permute-done = bf16[72,128]{1,0:T(8,128)(2,1)S(1)} collective-permute-done((bf16[72,128]{1,0:T(8,128)(2,1)S(1)}, bf16[72,128]{1,0:T(8,128)(2,1)S(1)}, u32[]{:S(2)}, u32[]{:S(2)}) %collective-permute-start) | collective-permute-done | bytes 18464 | tf_op jit(solution)/shard_map/ppermute | solution.py:531
  10.8 1.5 %collective-permute-start.3 = (bf16[288,128]{1,0:T(8,128)(2,1)S(1)}, bf16[288,128]{1,0:T(8,128)(2,1)S(1)}, u32[]{:S(2)}, u32[]{:S(2)}) collective-permute-start(bf16[288,128]{1,0:T(8,128)(2,1)S(1)} %pad_maximum_fusion.1), channel_id=1, source_target_pairs={{0,2},{1,3},{2,0},{3,1},{4,6},{5,7},{6,4},{7,5},{8,10},{9,11},{10,... | collective-permute-start | bytes 221192 | tf_op jit(solution)/shard_map/ppermute | solution.py:528
  12.2 1.6 %shard_map.119 = (f32[32,32,128]{2,1,0:T(8,128)S(1)}, bf16[2,256,128]{2,1,0:T(8,128)(2,1)S(1)}, f32[4,128]{1,0:T(4,128)S(1)}, bf16[4,1152,128]{2,1,0:T(8,128)(2,...) custom-call(s32[2]{0:T(128)} %refs_0_, bf16[2,256,128]{2,1,0:T(8,128)(2,1)} %refs_1_.1, ...), custom_call_target="tpu_custom_call" | custom-call | bytes 4194304 | tf_op jit(solution)/shard_map/pallas_call | solution.py:542
  13.8 1.3 %collective-permute-done.3 = bf16[288,128]{1,0:T(8,128)(2,1)S(1)} collective-permute-done((bf16[288,128]{1,0:T(8,128)(2,1)S(1)}, bf16[288,128]{1,0:T(8,128)(2,1)S(1)}, u32[]{:S(2)}, u32[]{:S(2)}) %collective-permute-start.3) | collective-permute-done | bytes 73760 | tf_op jit(solution)/shard_map/ppermute | solution.py:528
  15.1 0.1 collective-permute-start.4
  15.2 1.4 %collective-permute-done.4.refs_1_ = bf16[576,128]{1,0:T(8,128)(2,1)S(1)} collective-permute-done((bf16[576,128]{1,0:T(8,128)(2,1)S(1)}, bf16[576,128]{1,0:T(8,128)(2,1)S(1)}, u32[]{:S(2)}, u32[]{:S(2)}) %collective-permute-start.4) | collective-permute-done | bytes 147488 | tf_op jit(solution)/shard_map/ppermute | solution.py:528
  16.6 7.3 %shard_map.120 = (bf16[8,8,128]{2,1,0:T(8,128)(2,1)}, f32[2,256]{1,0:T(2,128)}, f32[2,256,128]{2,1,0:T(8,128)}, f32[4,128]{1,0:T(4,128)}, f32[4,9,128,128]{3,2,1,0:T(8,128)}, /*index=5*/f32[4,128,128]{2,1,0:T(8,128)}) custom-call(bf16[576,128]{1,0:T(8,128)(2,1)S(1)} %pad_maximum_fusion.refs_0_, bf16[576,128]{1,0:T(8,128)(2,1)S(1)} %collective-permute-done.4.refs_1_, ...), custom_call_target="tpu_custom_call" | custom-call | tf_op jit(solution)/shard_map/pallas_call | solution.py:569
  (2 shorter events, 0.0 us)
Async XLA Ops:
  1.4 7.0 %collective-permute-start.2 = (bf16[72,128]{1,0:T(8,128)(2,1)S(1)}, bf16[72,128]{1,0:T(8,128)(2,1)S(1)}, u32[]{:S(2)}, u32[]{:S(2)}) collective-permute-start(bf16[72,128]{1,0:T(8,128)(2,1)S(1)} %shard_map.118), channel_id=1, source_target_pairs={{0,4},{4,8},{8,12},{12,0},{1,5},{5,9},{9,13},{13,1},{2,6},{6,10},{... | collective-permute-start | bytes 55304 | tf_op jit(solution)/shard_map/ppermute | solution.py:531
  4.4 4.8 %collective-permute-start.1 = (bf16[72,128]{1,0:T(8,128)(2,1)S(1)}, bf16[72,128]{1,0:T(8,128)(2,1)S(1)}, u32[]{:S(2)}, u32[]{:S(2)}) collective-permute-start(bf16[72,128]{1,0:T(8,128)(2,1)S(1)} %shard_map.118), channel_id=1, source_target_pairs={{0,8},{4,12},{8,0},{12,4},{1,9},{5,13},{9,1},{13,5},{2,10},{6,14},... | collective-permute-start | bytes 55304 | tf_op jit(solution)/shard_map/ppermute | solution.py:531
  7.0 3.8 %collective-permute-start = (bf16[72,128]{1,0:T(8,128)(2,1)S(1)}, bf16[72,128]{1,0:T(8,128)(2,1)S(1)}, u32[]{:S(2)}, u32[]{:S(2)}) collective-permute-start(bf16[72,128]{1,0:T(8,128)(2,1)S(1)} %shard_map.118), channel_id=1, source_target_pairs={{0,12},{4,0},{8,4},{12,8},{1,13},{5,1},{9,5},{13,9},{2,14},{6,2},{... | collective-permute-start | bytes 55304 | tf_op jit(solution)/shard_map/ppermute | solution.py:531
  10.8 4.4 %collective-permute-start.3 = (bf16[288,128]{1,0:T(8,128)(2,1)S(1)}, bf16[288,128]{1,0:T(8,128)(2,1)S(1)}, u32[]{:S(2)}, u32[]{:S(2)}) collective-permute-start(bf16[288,128]{1,0:T(8,128)(2,1)S(1)} %pad_maximum_fusion.1), channel_id=1, source_target_pairs={{0,2},{1,3},{2,0},{3,1},{4,6},{5,7},{6,4},{7,5},{8,10},{9,11},{10,... | collective-permute-start | bytes 221192 | tf_op jit(solution)/shard_map/ppermute | solution.py:528
  15.1 1.4 %collective-permute-start.4 = (bf16[576,128]{1,0:T(8,128)(2,1)S(1)}, bf16[576,128]{1,0:T(8,128)(2,1)S(1)}, u32[]{:S(2)}, u32[]{:S(2)}) collective-permute-start(bf16[576,128]{1,0:T(8,128)(2,1)S(1)} %pad_maximum_fusion.refs_0_), channel_id=1, source_target_pairs={{0,1},{1,0},{2,3},{3,2},{4,5},{5,4},{6,7},{7,6},{8,9},{9,8},{10,11... | collective-permute-start | bytes 442376 | tf_op jit(solution)/shard_map/ppermute | solution.py:528

commit v5 on v4

--- a/solution.py
+++ b/solution.py
@@ -232,6 +232,24 @@
 
 def mix_parts(height):
     return [slice(0, height)]
+
+
+def ring_order(size):
+    return list(range(0, size, 2)) + list(range(1, size, 2))
+
+
+def ring_place(member, size):
+    half, odd = (size + 1) // 2, lax.rem(member, 2)
+    return lax.div(member, 2) + half * odd
+
+
+def ring_member(place, size):
+    half = (size + 1) // 2
+    return jnp.where(place < half, 2 * place, 2 * (place - half) + 1)
+
+
+def turn_order(size):
+    return list(range(2, size)) + [1]
 
 
 def in_hbm(x):
@@ -326,10 +344,12 @@
 
     piece_rows = pieces[0].shape[0] // (2 * grid_rows)
     tile = tile_rows * tile_cols
+    turns = [0] + turn_order(grid_rows)
     for step_col in range(grid_cols):
         source_col = lax.bitwise_xor(col, step_col)
         for step_row in range(grid_rows):
-            source_row = lax.rem(row + step_row, grid_rows)
+            place = lax.rem(ring_place(row, grid_rows) + grid_rows - turns[step_row], grid_rows)
+            source_row = ring_member(place, grid_rows)
             first = (step_col // 2 * grid_rows + step_row) * piece_rows
             piece = pieces[step_col % 2][first : first + piece_rows, :].astype(jnp.float32)
             back[
@@ -527,10 +547,15 @@
     def swap(x, axis, count, bit):
         return lax.ppermute(x, axis, [(i, i ^ bit) for i in range(count)])
 
-    def rotate(x, axis, count, step):
-        return lax.ppermute(x, axis, [(i, (i + step) % count) for i in range(count)])
-
-    turns = [rotate(payload, "row", grid_rows, k) for k in reversed(range(1, grid_rows))]
+    ring = ring_order(grid_rows)
+    turns = [
+        lax.ppermute(
+            payload,
+            "row",
+            [(ring[i], ring[(i + k) % grid_rows]) for i in range(grid_rows)],
+        )
+        for k in turn_order(grid_rows)
+    ]
     column = lax.optimization_barrier(jnp.concatenate([payload] + turns, axis=0))
     column, lengths = lax.optimization_barrier((column, lengths))
     held = (
@@ -605,9 +630,17 @@
     )
 
 
+def map_fits(grid_cols, tile_rows, residues, channels):
+    height = most_live(residues)
+    held = height * height * channels * LAYERS * 24
+    return grid_cols == 4 and tile_rows % 8 == 0 and height % CHUNK == 0 and held <= 16 * 2**20
+
+
 def body(seq_feat, lengths, embed_weight, norm_gain, conv_weight, proj_weight, pair_cotangent):
-    residues = pair_cotangent.shape[0] * lax.axis_size("row")
-    plan = replicated_body if residues <= 32 else tiled_body
+    tile_rows, _, channels = pair_cotangent.shape
+    residues = tile_rows * lax.axis_size("row")
+    whole = map_fits(lax.axis_size("col"), tile_rows, residues, channels)
+    plan = replicated_body if whole else tiled_body
     return plan(
         seq_feat, lengths, embed_weight, norm_gain, conv_weight, proj_weight, pair_cotangent
     )

time: 24.1 us -> 23.6 us (0.979)
  starting transfers between devices: 8.52 us -> 7.32 us
  waiting for transfers between devices: 5.07 us -> 5.8 us
    ppermute x3, starting transfers between devices: 6.96 us -> 5.62 us  [replicated_body(): lax.ppermute(payload, 'row', [(ring[i], ring[(i + k) % grid_rows]) for i...]
    ppermute x3, waiting for transfers between devices: 2.41 us -> 3.28 us  [replicated_body(): lax.ppermute(payload, 'row', [(ring[i], ring[(i + k) % grid_rows]) for i...]
  transfers between devices with their start and end apart: 5 -> 5, of which waited for: 4 -> 5; matrix products, arithmetic and copies ran while one was open for 0% -> 0% of each run, Pallas kernels for 7% -> 7%
where the time goes in v5:
time: 23.6 us; the launch traced here: 23.4 us
  Pallas kernels  9.61 us (41%)
  starting transfers between devices  7.32 us (31%)
  waiting for transfers between devices  5.8 us (25%)
  between operations  0.66 us (3%)
    pallas_call x1, Pallas kernels, replicated_body(): pl.pallas_call(functools.partial(block_kernel, grid_rows, grid_cols), out...  7.31 us
    ppermute x3, starting transfers between devices, replicated_body(): lax.ppermute(payload, 'row', [(ring[i], ring[(i + k) % grid_rows]) for i...  5.62 us
    ppermute x3, waiting for transfers between devices, replicated_body(): lax.ppermute(payload, 'row', [(ring[i], ring[(i + k) % grid_rows]) for i...  3.28 us
    ppermute x2, waiting for transfers between devices, swap(): return lax.ppermute(x, axis, [(i, i ^ bit) for i in range(count)])  2.53 us
    ppermute x2, starting transfers between devices, swap(): return lax.ppermute(x, axis, [(i, i ^ bit) for i in range(count)])  1.7 us
    pallas_call x1, Pallas kernels, replicated_body(): pl.pallas_call(setup_kernel, out_shape=[pltpu.VMEM(square, f32)] + [pltpu...  1.56 us
    pallas_call x1, Pallas kernels, replicated_body(): pl.pallas_call(pack_kernel, out_shape=pltpu.VMEM((tile_rows * tile_cols +...  0.74 us
  transfers between devices with their start and end apart: 5, of which 5 were waited for; matrix products, arithmetic and copies ran while one was open for 0% of the time, Pallas kernels for 7%

profile of v5, /device:TPU:0, one launch (start us, length us, event | category | flops | bytes accessed | tf_op | source)
XLA Modules:
  0.0 23.4 jit_solution(4807522240270877694)
XLA Ops:
  0.6 0.7 %shard_map.118 = bf16[72,128]{1,0:T(8,128)(2,1)S(1)} custom-call(bf16[2,256]{1,0:T(2,128)(2,1)} %seq_ref.1, bf16[8,8,128]{2,1,0:T(8,128)(2,1)} %tile_ref.1), custom_call_target="tpu_custom_call" | custom-call | tf_op jit(solution)/shard_map/pallas_call | solution.py:542
  1.4 4.0 %collective-permute-start.2 = (bf16[72,128]{1,0:T(8,128)(2,1)S(1)}, bf16[72,128]{1,0:T(8,128)(2,1)S(1)}, u32[]{:S(2)}, u32[]{:S(2)}) collective-permute-start(bf16[72,128]{1,0:T(8,128)(2,1)S(1)} %shard_map.118), channel_id=1, source_target_pairs={{0,8},{8,4},{4,12},{12,0},{1,9},{9,5},{5,13},{13,1},{2,10},{10,6},... | collective-permute-start | bytes 55304 | tf_op jit(solution)/shard_map/ppermute | solution.py:552
  5.4 1.1 %collective-permute-start.1 = (bf16[72,128]{1,0:T(8,128)(2,1)S(1)}, bf16[72,128]{1,0:T(8,128)(2,1)S(1)}, u32[]{:S(2)}, u32[]{:S(2)}) collective-permute-start(bf16[72,128]{1,0:T(8,128)(2,1)S(1)} %shard_map.118), channel_id=1, source_target_pairs={{0,12},{8,0},{4,8},{12,4},{1,13},{9,1},{5,9},{13,5},{2,14},{10,2},... | collective-permute-start | bytes 55304 | tf_op jit(solution)/shard_map/ppermute | solution.py:552
  6.5 0.5 %collective-permute-start = (bf16[72,128]{1,0:T(8,128)(2,1)S(1)}, bf16[72,128]{1,0:T(8,128)(2,1)S(1)}, u32[]{:S(2)}, u32[]{:S(2)}) collective-permute-start(bf16[72,128]{1,0:T(8,128)(2,1)S(1)} %shard_map.118), channel_id=1, source_target_pairs={{0,4},{8,12},{4,0},{12,8},{1,5},{9,13},{5,1},{13,9},{2,6},{10,14},... | collective-permute-start | bytes 55304 | tf_op jit(solution)/shard_map/ppermute | solution.py:552
  7.0 1.2 %collective-permute-done.2 = bf16[72,128]{1,0:T(8,128)(2,1)S(1)} collective-permute-done((bf16[72,128]{1,0:T(8,128)(2,1)S(1)}, bf16[72,128]{1,0:T(8,128)(2,1)S(1)}, u32[]{:S(2)}, u32[]{:S(2)}) %collective-permute-start.2) | collective-permute-done | bytes 18464 | tf_op jit(solution)/shard_map/ppermute | solution.py:552
  8.2 1.9 %collective-permute-done.1 = bf16[72,128]{1,0:T(8,128)(2,1)S(1)} collective-permute-done((bf16[72,128]{1,0:T(8,128)(2,1)S(1)}, bf16[72,128]{1,0:T(8,128)(2,1)S(1)}, u32[]{:S(2)}, u32[]{:S(2)}) %collective-permute-start.1) | collective-permute-done | bytes 18464 | tf_op jit(solution)/shard_map/ppermute | solution.py:552
  10.1 0.2 collective-permute-done
  10.3 1.6 %collective-permute-start.3 = (bf16[288,128]{1,0:T(8,128)(2,1)S(1)}, bf16[288,128]{1,0:T(8,128)(2,1)S(1)}, u32[]{:S(2)}, u32[]{:S(2)}) collective-permute-start(bf16[288,128]{1,0:T(8,128)(2,1)S(1)} %pad_maximum_fusion.1), channel_id=1, source_target_pairs={{0,2},{1,3},{2,0},{3,1},{4,6},{5,7},{6,4},{7,5},{8,10},{9,11},{10,... | collective-permute-start | bytes 221192 | tf_op jit(solution)/shard_map/ppermute | solution.py:548
  11.9 1.6 %shard_map.119 = (f32[32,32,128]{2,1,0:T(8,128)S(1)}, bf16[2,256,128]{2,1,0:T(8,128)(2,1)S(1)}, f32[4,128]{1,0:T(4,128)S(1)}, bf16[4,1152,128]{2,1,0:T(8,128)(2,...) custom-call(s32[2]{0:T(128)} %refs_0_, bf16[2,256,128]{2,1,0:T(8,128)(2,1)} %refs_1_.1, ...), custom_call_target="tpu_custom_call" | custom-call | bytes 4194304 | tf_op jit(solution)/shard_map/pallas_call | solution.py:567
  13.5 1.2 %collective-permute-done.3 = bf16[288,128]{1,0:T(8,128)(2,1)S(1)} collective-permute-done((bf16[288,128]{1,0:T(8,128)(2,1)S(1)}, bf16[288,128]{1,0:T(8,128)(2,1)S(1)}, u32[]{:S(2)}, u32[]{:S(2)}) %collective-permute-start.3) | collective-permute-done | bytes 73760 | tf_op jit(solution)/shard_map/ppermute | solution.py:548
  14.7 0.1 collective-permute-start.4
  14.7 1.4 %collective-permute-done.4.refs_1_ = bf16[576,128]{1,0:T(8,128)(2,1)S(1)} collective-permute-done((bf16[576,128]{1,0:T(8,128)(2,1)S(1)}, bf16[576,128]{1,0:T(8,128)(2,1)S(1)}, u32[]{:S(2)}, u32[]{:S(2)}) %collective-permute-start.4) | collective-permute-done | bytes 147488 | tf_op jit(solution)/shard_map/ppermute | solution.py:548
  16.1 7.3 %shard_map.120 = (bf16[8,8,128]{2,1,0:T(8,128)(2,1)}, f32[2,256]{1,0:T(2,128)}, f32[2,256,128]{2,1,0:T(8,128)}, f32[4,128]{1,0:T(4,128)}, f32[4,9,128,128]{3,2,1,0:T(8,128)}, /*index=5*/f32[4,128,128]{2,1,0:T(8,128)}) custom-call(bf16[576,128]{1,0:T(8,128)(2,1)S(1)} %pad_maximum_fusion.refs_0_, bf16[576,128]{1,0:T(8,128)(2,1)S(1)} %collective-permute-done.4.refs_1_, ...), custom_call_target="tpu_custom_call" | custom-call | tf_op jit(solution)/shard_map/pallas_call | solution.py:594
  (2 shorter events, 0.0 us)
Async XLA Ops:
  1.4 6.8 %collective-permute-start.2 = (bf16[72,128]{1,0:T(8,128)(2,1)S(1)}, bf16[72,128]{1,0:T(8,128)(2,1)S(1)}, u32[]{:S(2)}, u32[]{:S(2)}) collective-permute-start(bf16[72,128]{1,0:T(8,128)(2,1)S(1)} %shard_map.118), channel_id=1, source_target_pairs={{0,8},{8,4},{4,12},{12,0},{1,9},{9,5},{5,13},{13,1},{2,10},{10,6},... | collective-permute-start | bytes 55304 | tf_op jit(solution)/shard_map/ppermute | solution.py:552
  5.4 4.7 %collective-permute-start.1 = (bf16[72,128]{1,0:T(8,128)(2,1)S(1)}, bf16[72,128]{1,0:T(8,128)(2,1)S(1)}, u32[]{:S(2)}, u32[]{:S(2)}) collective-permute-start(bf16[72,128]{1,0:T(8,128)(2,1)S(1)} %shard_map.118), channel_id=1, source_target_pairs={{0,12},{8,0},{4,8},{12,4},{1,13},{9,1},{5,9},{13,5},{2,14},{10,2},... | collective-permute-start | bytes 55304 | tf_op jit(solution)/shard_map/ppermute | solution.py:552
  6.5 3.8 %collective-permute-start = (bf16[72,128]{1,0:T(8,128)(2,1)S(1)}, bf16[72,128]{1,0:T(8,128)(2,1)S(1)}, u32[]{:S(2)}, u32[]{:S(2)}) collective-permute-start(bf16[72,128]{1,0:T(8,128)(2,1)S(1)} %shard_map.118), channel_id=1, source_target_pairs={{0,4},{8,12},{4,0},{12,8},{1,5},{9,13},{5,1},{13,9},{2,6},{10,14},... | collective-permute-start | bytes 55304 | tf_op jit(solution)/shard_map/ppermute | solution.py:552
  10.3 4.4 %collective-permute-start.3 = (bf16[288,128]{1,0:T(8,128)(2,1)S(1)}, bf16[288,128]{1,0:T(8,128)(2,1)S(1)}, u32[]{:S(2)}, u32[]{:S(2)}) collective-permute-start(bf16[288,128]{1,0:T(8,128)(2,1)S(1)} %pad_maximum_fusion.1), channel_id=1, source_target_pairs={{0,2},{1,3},{2,0},{3,1},{4,6},{5,7},{6,4},{7,5},{8,10},{9,11},{10,... | collective-permute-start | bytes 221192 | tf_op jit(solution)/shard_map/ppermute | solution.py:548
  14.7 1.4 %collective-permute-start.4 = (bf16[576,128]{1,0:T(8,128)(2,1)S(1)}, bf16[576,128]{1,0:T(8,128)(2,1)S(1)}, u32[]{:S(2)}, u32[]{:S(2)}) collective-permute-start(bf16[576,128]{1,0:T(8,128)(2,1)S(1)} %pad_maximum_fusion.refs_0_), channel_id=1, source_target_pairs={{0,1},{1,0},{2,3},{3,2},{4,5},{5,4},{6,7},{7,6},{8,9},{9,8},{10,11... | collective-permute-start | bytes 442376 | tf_op jit(solution)/shard_map/ppermute | solution.py:548

commit v6 on v5

--- a/solution.py
+++ b/solution.py
@@ -227,7 +227,7 @@
     return residues - residues // 4
 
 
-CHUNK = 8
+CHUNK = 24
 
 
 def mix_parts(height):
@@ -291,7 +291,7 @@
 
 
 def block_kernel(grid_rows, grid_cols, *refs):
-    pieces, refs = refs[:2], refs[2:]
+    pieces, refs = (refs[0], refs[2], refs[3], refs[1]), refs[4:]
     live, embed, gains, weights, proj, proj_mean = refs[:6]
     (pair_hbm, seq_grad_hbm, embed_grad_hbm, gain_grad_hbm, conv_grad_hbm, proj_grad_hbm) = refs[6:12]
     (
@@ -336,13 +336,16 @@
         copy.start()
         stores.append(copy)
 
-    stream[...] = jnp.zeros_like(stream)
-    shifted[...] = jnp.zeros_like(shifted)
+    dead = residues - height
+    stream[height:, :, :] = jnp.zeros((dead, residues, channels), jnp.float32)
+    stream[:height, height:, :] = jnp.zeros((height, dead, channels), jnp.float32)
+    shifted[:, :margin, :] = jnp.zeros((height, margin, channels), jnp.float32)
+    shifted[:, margin + height :, :] = jnp.zeros((height, margin, channels), jnp.float32)
     for ref in (taps, mixed):
         ref[:pad, :] = jnp.zeros((pad, ref.shape[1]), ref.dtype)
         ref[pad + count :, :] = jnp.zeros((pad, ref.shape[1]), ref.dtype)
 
-    piece_rows = pieces[0].shape[0] // (2 * grid_rows)
+    piece_rows = pieces[0].shape[0] // grid_rows
     tile = tile_rows * tile_cols
     turns = [0] + turn_order(grid_rows)
     for step_col in range(grid_cols):
@@ -350,8 +353,8 @@
         for step_row in range(grid_rows):
             place = lax.rem(ring_place(row, grid_rows) + grid_rows - turns[step_row], grid_rows)
             source_row = ring_member(place, grid_rows)
-            first = (step_col // 2 * grid_rows + step_row) * piece_rows
-            piece = pieces[step_col % 2][first : first + piece_rows, :].astype(jnp.float32)
+            first = step_row * piece_rows
+            piece = pieces[step_col][first : first + piece_rows, :].astype(jnp.float32)
             back[
                 pl.ds(pl.multiple_of(source_row * tile_rows, tile_rows), tile_rows),
                 pl.ds(pl.multiple_of(source_col * tile_cols, tile_cols), tile_cols),
@@ -485,6 +488,14 @@
         )
         for part in mix_parts(height):
             mix(part, wide, NT)
+        proj_grad_ref[layer] = dot(excited[layer], masked[...], TN) * grad_scale
+        every = slice(0, count)
+        for a in (-1, 0, 1):
+            part_grad = dot(squashed[layer], taps[moved(every, -a * spacing), :], TN) * grad_scale
+            for b in range(3):
+                conv_grad[layer, 3 * (a + 1) + b] = part_grad[:, b * channels : (b + 1) * channels]
+        store(conv_grad.at[layer], conv_grad_hbm.at[layer], grad_sem.at[0, layer])
+        store(proj_grad_ref.at[layer], proj_grad_hbm.at[layer], grad_sem.at[1, layer])
         gain_total = jnp.zeros((1, channels), jnp.float32)
         for part in chunks:
             rows = flat(part)
@@ -497,14 +508,6 @@
             )
             put(back, part, get(back, part) + delta)
         gain_grad_ref[layer : layer + 1, :] = gain_total * grad_scale
-        proj_grad_ref[layer] = dot(excited[layer], masked[...], TN) * grad_scale
-        every = slice(0, count)
-        for a in (-1, 0, 1):
-            part_grad = dot(squashed[layer], taps[moved(every, -a * spacing), :], TN) * grad_scale
-            for b in range(3):
-                conv_grad[layer, 3 * (a + 1) + b] = part_grad[:, b * channels : (b + 1) * channels]
-        store(conv_grad.at[layer], conv_grad_hbm.at[layer], grad_sem.at[0, layer])
-        store(proj_grad_ref.at[layer], proj_grad_hbm.at[layer], grad_sem.at[1, layer])
 
     final = back[:height, :height, :]
     rest = jnp.zeros((residues - height, channels), jnp.float32)
@@ -576,10 +579,7 @@
         cost_estimate=pl.CostEstimate(flops=0, bytes_accessed=4 * 2**20, transcendentals=0),
     )(in_hbm(lengths), *[in_hbm(x) for x in held])
 
-    chip = [column, swap(column, "col", grid_cols, 2)]
-    chip, live, held = lax.optimization_barrier((chip, live, held))
-    chip = lax.optimization_barrier(jnp.concatenate(chip, axis=0))
-    pieces = [chip, swap(chip, "col", grid_cols, 1)]
+    pieces = [column] + [swap(column, "col", grid_cols, k) for k in (3, 1, 2)]
     count = height * height
     edge = margin * height
     saved = (LAYERS, count, channels)
@@ -594,7 +594,7 @@
     outs = pl.pallas_call(
         functools.partial(block_kernel, grid_rows, grid_cols),
         out_shape=results,
-        in_specs=[vmem] * 8,
+        in_specs=[vmem] * 10,
         out_specs=(hbm,) * len(results),
         scratch_shapes=[
             pltpu.VMEM(square, f32),

time: 23.6 us -> 23.3 us (0.987)
  waiting for transfers between devices: 5.8 us -> 5.11 us
  starting transfers between devices: 7.32 us -> 7.77 us
    ppermute x2 -> x3, waiting for transfers between devices: 2.53 us -> 1.84 us  [swap(): return lax.ppermute(x, axis, [(i, i ^ bit) for i in range(count)])]
    ppermute x2 -> x3, starting transfers between devices: 1.7 us -> 2.15 us  [swap(): return lax.ppermute(x, axis, [(i, i ^ bit) for i in range(count)])]
  transfers between devices with their start and end apart: 5 -> 6, of which waited for: 5 -> 5; matrix products, arithmetic and copies ran while one was open for 0% -> 0% of each run, Pallas kernels for 7% -> 7%
where the time goes in v6:
time: 23.3 us; the launch traced here: 23.1 us
  Pallas kernels  9.54 us (41%)
  starting transfers between devices  7.77 us (33%)
  waiting for transfers between devices  5.11 us (22%)
  between operations  0.65 us (3%)
    pallas_call x1, Pallas kernels, replicated_body(): pl.pallas_call(functools.partial(block_kernel, grid_rows, grid_cols), out...  7.24 us
    ppermute x3, starting transfers between devices, replicated_body(): lax.ppermute(payload, 'row', [(ring[i], ring[(i + k) % grid_rows]) for i...  5.62 us
    ppermute x3, waiting for transfers between devices, replicated_body(): lax.ppermute(payload, 'row', [(ring[i], ring[(i + k) % grid_rows]) for i...  3.28 us
    ppermute x3, starting transfers between devices, swap(): return lax.ppermute(x, axis, [(i, i ^ bit) for i in range(count)])  2.15 us
    ppermute x3, waiting for transfers between devices, swap(): return lax.ppermute(x, axis, [(i, i ^ bit) for i in range(count)])  1.84 us
    pallas_call x1, Pallas kernels, replicated_body(): pl.pallas_call(setup_kernel, out_shape=[pltpu.VMEM(square, f32)] + [pltpu...  1.56 us
    pallas_call x1, Pallas kernels, replicated_body(): pl.pallas_call(pack_kernel, out_shape=pltpu.VMEM((tile_rows * tile_cols +...  0.74 us
  transfers between devices with their start and end apart: 6, of which 5 were waited for; matrix products, arithmetic and copies ran while one was open for 0% of the time, Pallas kernels for 7%

profile of v6, /device:TPU:0, one launch (start us, length us, event | category | flops | bytes accessed | tf_op | source)
XLA Modules:
  0.0 23.1 jit_solution(3165457866215317524)
XLA Ops:
  0.6 0.7 %shard_map.118 = bf16[72,128]{1,0:T(8,128)(2,1)S(1)} custom-call(bf16[2,256]{1,0:T(2,128)(2,1)} %seq_ref.1, bf16[8,8,128]{2,1,0:T(8,128)(2,1)} %tile_ref.1), custom_call_target="tpu_custom_call" | custom-call | tf_op jit(solution)/shard_map/pallas_call | solution.py:545
  1.4 4.0 %collective-permute-start.2 = (bf16[72,128]{1,0:T(8,128)(2,1)S(1)}, bf16[72,128]{1,0:T(8,128)(2,1)S(1)}, u32[]{:S(2)}, u32[]{:S(2)}) collective-permute-start(bf16[72,128]{1,0:T(8,128)(2,1)S(1)} %shard_map.118), channel_id=1, source_target_pairs={{0,8},{8,4},{4,12},{12,0},{1,9},{9,5},{5,13},{13,1},{2,10},{10,6},... | collective-permute-start | bytes 55304 | tf_op jit(solution)/shard_map/ppermute | solution.py:555
  5.4 1.1 %collective-permute-start.1 = (bf16[72,128]{1,0:T(8,128)(2,1)S(1)}, bf16[72,128]{1,0:T(8,128)(2,1)S(1)}, u32[]{:S(2)}, u32[]{:S(2)}) collective-permute-start(bf16[72,128]{1,0:T(8,128)(2,1)S(1)} %shard_map.118), channel_id=1, source_target_pairs={{0,12},{8,0},{4,8},{12,4},{1,13},{9,1},{5,9},{13,5},{2,14},{10,2},... | collective-permute-start | bytes 55304 | tf_op jit(solution)/shard_map/ppermute | solution.py:555
  6.5 0.5 %collective-permute-start = (bf16[72,128]{1,0:T(8,128)(2,1)S(1)}, bf16[72,128]{1,0:T(8,128)(2,1)S(1)}, u32[]{:S(2)}, u32[]{:S(2)}) collective-permute-start(bf16[72,128]{1,0:T(8,128)(2,1)S(1)} %shard_map.118), channel_id=1, source_target_pairs={{0,4},{8,12},{4,0},{12,8},{1,5},{9,13},{5,1},{13,9},{2,6},{10,14},... | collective-permute-start | bytes 55304 | tf_op jit(solution)/shard_map/ppermute | solution.py:555
  7.0 1.2 %collective-permute-done.2 = bf16[72,128]{1,0:T(8,128)(2,1)S(1)} collective-permute-done((bf16[72,128]{1,0:T(8,128)(2,1)S(1)}, bf16[72,128]{1,0:T(8,128)(2,1)S(1)}, u32[]{:S(2)}, u32[]{:S(2)}) %collective-permute-start.2) | collective-permute-done | bytes 18464 | tf_op jit(solution)/shard_map/ppermute | solution.py:555
  8.2 1.9 %collective-permute-done.1 = bf16[72,128]{1,0:T(8,128)(2,1)S(1)} collective-permute-done((bf16[72,128]{1,0:T(8,128)(2,1)S(1)}, bf16[72,128]{1,0:T(8,128)(2,1)S(1)}, u32[]{:S(2)}, u32[]{:S(2)}) %collective-permute-start.1) | collective-permute-done | bytes 18464 | tf_op jit(solution)/shard_map/ppermute | solution.py:555
  10.1 0.2 collective-permute-done
  10.3 1.6 %collective-permute-start.5 = (bf16[288,128]{1,0:T(8,128)(2,1)S(1)}, bf16[288,128]{1,0:T(8,128)(2,1)S(1)}, u32[]{:S(2)}, u32[]{:S(2)}) collective-permute-start(bf16[288,128]{1,0:T(8,128)(2,1)S(1)} %pad_maximum_fusion.refs_0_), channel_id=1, source_target_pairs={{0,2},{1,3},{2,0},{3,1},{4,6},{5,7},{6,4},{7,5},{8,10},{9,11},{10,... | collective-permute-start | bytes 221192 | tf_op jit(solution)/shard_map/ppermute | solution.py:551
  11.9 0.0 collective-permute-start.4
  11.9 0.5 %collective-permute-start.3 = (bf16[288,128]{1,0:T(8,128)(2,1)S(1)}, bf16[288,128]{1,0:T(8,128)(2,1)S(1)}, u32[]{:S(2)}, u32[]{:S(2)}) collective-permute-start(bf16[288,128]{1,0:T(8,128)(2,1)S(1)} %pad_maximum_fusion.refs_0_), channel_id=1, source_target_pairs={{0,3},{1,2},{2,1},{3,0},{4,7},{5,6},{6,5},{7,4},{8,11},{9,10},{10,... | collective-permute-start | bytes 221192 | tf_op jit(solution)/shard_map/ppermute | solution.py:551
  12.4 1.6 %shard_map.119 = (f32[32,32,128]{2,1,0:T(8,128)S(1)}, bf16[2,256,128]{2,1,0:T(8,128)(2,1)S(1)}, f32[4,128]{1,0:T(4,128)S(1)}, bf16[4,1152,128]{2,1,0:T(8,128)(2,...) custom-call(s32[2]{0:T(128)} %refs_0_, bf16[2,256,128]{2,1,0:T(8,128)(2,1)} %refs_1_.1, ...), custom_call_target="tpu_custom_call" | custom-call | bytes 4194304 | tf_op jit(solution)/shard_map/pallas_call | solution.py:570
  14.0 0.6 %collective-permute-done.5.refs_3_ = bf16[288,128]{1,0:T(8,128)(2,1)S(1)} collective-permute-done((bf16[288,128]{1,0:T(8,128)(2,1)S(1)}, bf16[288,128]{1,0:T(8,128)(2,1)S(1)}, u32[]{:S(2)}, u32[]{:S(2)}) %collective-permute-start.5) | collective-permute-done | bytes 73760 | tf_op jit(solution)/shard_map/ppermute | solution.py:551
  14.6 0.0 collective-permute-done.4.refs_2_
  14.6 1.2 %collective-permute-done.3.refs_1_ = bf16[288,128]{1,0:T(8,128)(2,1)S(1)} collective-permute-done((bf16[288,128]{1,0:T(8,128)(2,1)S(1)}, bf16[288,128]{1,0:T(8,128)(2,1)S(1)}, u32[]{:S(2)}, u32[]{:S(2)}) %collective-permute-start.3) | collective-permute-done | bytes 73760 | tf_op jit(solution)/shard_map/ppermute | solution.py:551
  15.8 7.2 %shard_map.120 = (bf16[8,8,128]{2,1,0:T(8,128)(2,1)}, f32[2,256]{1,0:T(2,128)}, f32[2,256,128]{2,1,0:T(8,128)}, f32[4,128]{1,0:T(4,128)}, f32[4,9,128,128]{3,2,1,0:T(8,128)}, /*index=5*/f32[4,128,128]{2,1,0:T(8,128)}) custom-call(bf16[288,128]{1,0:T(8,128)(2,1)S(1)} %pad_maximum_fusion.refs_0_, bf16[288,128]{1,0:T(8,128)(2,1)S(1)} %collective-permute-done.3.refs_1_, ...), custom_call_target="tpu_custom_call" | custom-call | tf_op jit(solution)/shard_map/pallas_call | solution.py:594
  (1 shorter events, 0.0 us)
Async XLA Ops:
  1.4 6.8 %collective-permute-start.2 = (bf16[72,128]{1,0:T(8,128)(2,1)S(1)}, bf16[72,128]{1,0:T(8,128)(2,1)S(1)}, u32[]{:S(2)}, u32[]{:S(2)}) collective-permute-start(bf16[72,128]{1,0:T(8,128)(2,1)S(1)} %shard_map.118), channel_id=1, source_target_pairs={{0,8},{8,4},{4,12},{12,0},{1,9},{9,5},{5,13},{13,1},{2,10},{10,6},... | collective-permute-start | bytes 55304 | tf_op jit(solution)/shard_map/ppermute | solution.py:555
  5.4 4.7 %collective-permute-start.1 = (bf16[72,128]{1,0:T(8,128)(2,1)S(1)}, bf16[72,128]{1,0:T(8,128)(2,1)S(1)}, u32[]{:S(2)}, u32[]{:S(2)}) collective-permute-start(bf16[72,128]{1,0:T(8,128)(2,1)S(1)} %shard_map.118), channel_id=1, source_target_pairs={{0,12},{8,0},{4,8},{12,4},{1,13},{9,1},{5,9},{13,5},{2,14},{10,2},... | collective-permute-start | bytes 55304 | tf_op jit(solution)/shard_map/ppermute | solution.py:555
  6.5 3.8 %collective-permute-start = (bf16[72,128]{1,0:T(8,128)(2,1)S(1)}, bf16[72,128]{1,0:T(8,128)(2,1)S(1)}, u32[]{:S(2)}, u32[]{:S(2)}) collective-permute-start(bf16[72,128]{1,0:T(8,128)(2,1)S(1)} %shard_map.118), channel_id=1, source_target_pairs={{0,4},{8,12},{4,0},{12,8},{1,5},{9,13},{5,1},{13,9},{2,6},{10,14},... | collective-permute-start | bytes 55304 | tf_op jit(solution)/shard_map/ppermute | solution.py:555
  10.3 4.4 %collective-permute-start.5 = (bf16[288,128]{1,0:T(8,128)(2,1)S(1)}, bf16[288,128]{1,0:T(8,128)(2,1)S(1)}, u32[]{:S(2)}, u32[]{:S(2)}) collective-permute-start(bf16[288,128]{1,0:T(8,128)(2,1)S(1)} %pad_maximum_fusion.refs_0_), channel_id=1, source_target_pairs={{0,2},{1,3},{2,0},{3,1},{4,6},{5,7},{6,4},{7,5},{8,10},{9,11},{10,... | collective-permute-start | bytes 221192 | tf_op jit(solution)/shard_map/ppermute | solution.py:551
  11.9 2.7 %collective-permute-start.4 = (bf16[288,128]{1,0:T(8,128)(2,1)S(1)}, bf16[288,128]{1,0:T(8,128)(2,1)S(1)}, u32[]{:S(2)}, u32[]{:S(2)}) collective-permute-start(bf16[288,128]{1,0:T(8,128)(2,1)S(1)} %pad_maximum_fusion.refs_0_), channel_id=1, source_target_pairs={{0,1},{1,0},{2,3},{3,2},{4,5},{5,4},{6,7},{7,6},{8,9},{9,8},{10,11... | collective-permute-start | bytes 221192 | tf_op jit(solution)/shard_map/ppermute | solution.py:551
  11.9 3.9 %collective-permute-start.3 = (bf16[288,128]{1,0:T(8,128)(2,1)S(1)}, bf16[288,128]{1,0:T(8,128)(2,1)S(1)}, u32[]{:S(2)}, u32[]{:S(2)}) collective-permute-start(bf16[288,128]{1,0:T(8,128)(2,1)S(1)} %pad_maximum_fusion.refs_0_), channel_id=1, source_target_pairs={{0,3},{1,2},{2,1},{3,0},{4,7},{5,6},{6,5},{7,4},{8,11},{9,10},{10,... | collective-permute-start | bytes 221192 | tf_op jit(solution)/shard_map/ppermute | solution.py:551
